TPU v7x, 32 devices: a whole 2x2x4 slice. The times are simulated.
32 devices in a mesh: dp: 8 (over z, x), tensor: 4 (over y, core).
Axes of the slice: x: 2, y: 2, z: 4, core: 2. Of those that a mesh axis runs over, the one named last changes fastest.
Arguments:
- tokens: bfloat16 [16384, 1024], P(('dp', 'tensor')), may hold values from -6 to 6
- cotangent: bfloat16 [16384, 1024], P(('dp', 'tensor')), may hold values from -6 to 6
- lengths: int32 [8, 16], P('dp'), may hold values from 1 to 256, 2048 in all within a row
- qkv_master: float32 [1024, 3, 1024], P('dp', None, 'tensor'), may hold values from -0.1875 to 0.1875
- qkv_first: float32 [1024, 3, 1024], P('dp', None, 'tensor'), may hold values from -0.00015258789 to 0.00015258789
- qkv_second: float32 [1024, 3, 1024], P('dp', None, 'tensor'), may hold values from 2.9798684e-11 to 4.7677895e-10
- out_master: float32 [1024, 1024], P(('tensor', 'dp')), may hold values from -1 to 1
- out_first: float32 [1024, 1024], P(('tensor', 'dp')), may hold values from -9.1552734e-05 to 9.1552734e-05
- out_second: float32 [1024, 1024], P(('tensor', 'dp')), may hold values from 5.959737e-12 to 9.535579e-11
- in_master: float32 [1024, 2, 4096], P('dp', None, 'tensor'), may hold values from -0.1875 to 0.1875
- in_first: float32 [1024, 2, 4096], P('dp', None, 'tensor'), may hold values from -0.00015258789 to 0.00015258789
- in_second: float32 [1024, 2, 4096], P('dp', None, 'tensor'), may hold values from 2.9798684e-11 to 4.7677895e-10
- down_master: float32 [4096, 1024], P(('tensor', 'dp')), may hold values from -0.09375 to 0.09375
- down_first: float32 [4096, 1024], P(('tensor', 'dp')), may hold values from -0.00015258789 to 0.00015258789
- down_second: float32 [4096, 1024], P(('tensor', 'dp')), may hold values from 2.9798684e-11 to 4.7677895e-10
- norm_gains: float32 [2, 1024], replicated, may hold values from 0.2 to 2.8
- gain_first: float32 [2, 1024], replicated, may hold values from -0.00061035156 to 0.00061035156
- gain_second: float32 [2, 1024], replicated, may hold values from 4.7677895e-10 to 7.628463e-09
Outputs:
- layer_out: bfloat16 [16384, 1024], P(('dp', 'tensor'))
- input_grad: float32 [16384, 1024], P(('dp', 'tensor'))
- qkv_grad: float32 [1024, 3, 1024], P('dp', None, 'tensor')
- qkv_new: float32 [1024, 3, 1024], P('dp', None, 'tensor')
- qkv_first_new: float32 [1024, 3, 1024], P('dp', None, 'tensor')
- qkv_second_new: float32 [1024, 3, 1024], P('dp', None, 'tensor')
- out_grad: float32 [1024, 1024], P(('tensor', 'dp'))
- out_new: float32 [1024, 1024], P(('tensor', 'dp'))
- out_first_new: float32 [1024, 1024], P(('tensor', 'dp'))
- out_second_new: float32 [1024, 1024], P(('tensor', 'dp'))
- in_grad: float32 [1024, 2, 4096], P('dp', None, 'tensor')
- in_new: float32 [1024, 2, 4096], P('dp', None, 'tensor')
- in_first_new: float32 [1024, 2, 4096], P('dp', None, 'tensor')
- in_second_new: float32 [1024, 2, 4096], P('dp', None, 'tensor')
- down_grad: float32 [4096, 1024], P(('tensor', 'dp'))
- down_new: float32 [4096, 1024], P(('tensor', 'dp'))
- down_first_new: float32 [4096, 1024], P(('tensor', 'dp'))
- down_second_new: float32 [4096, 1024], P(('tensor', 'dp'))
- gain_grad: float32 [2, 1024], replicated
- gain_new: float32 [2, 1024], replicated
- gain_first_new: float32 [2, 1024], replicated
- gain_second_new: float32 [2, 1024], replicated
- grad_norm: float32 [], replicated
Inputs may be any that keep to these rules, and one draw needn't show every extreme that they name: Each row's 16 window lengths are positive, add up to 2048, and the longest is 256.
All inputs are finite; a program needn't handle non-finite values.
Results may differ from a plain program's by a relative error of at most 0.024.
Values may be sent and summed in bfloat16 or wider, within the bound.
No kernel may reach another device: no remote copies, remote signals or barrier semaphores. Data moves between devices by JAX's collectives and lax.ppermute only.
A program may use at most 192 MiB of HBM per device.

v0:
```python
from functools import partial
import math

import jax
import jax.numpy as jnp
from jax import lax
from jax.sharding import PartitionSpec as P

D = 1024
HEADS = 16
HEAD_DIM = 64
FF = 4096
ROW = 2048
STEP = 5


eps_norm = 1e-05
beta_one = 0.9
beta_two = 0.999
learn_rate = 0.05
gain_rate = 0.6
weight_decay = 0.1
adam_eps = 1e-08
max_norm = 1.0


def layer_norm(values, gain):
    centre = values - jnp.mean(values, axis=-1, keepdims=True)
    spread = jnp.mean(centre * centre, axis=-1, keepdims=True)
    return centre * lax.rsqrt(spread + eps_norm) * gain


def row_layout(lengths):
    seg_ends = jnp.cumsum(lengths, axis=-1)
    places = jnp.arange(ROW, dtype=jnp.int32)
    passed = (places[:, None] >= seg_ends[..., None, :]).astype(jnp.int32)
    segment = jnp.sum(passed, axis=-1)
    offset = places - jnp.sum(passed * lengths[..., None, :], axis=-1)
    return (segment, offset)


def rotary_tables(offset):
    half_dim = HEAD_DIM // 2
    inverse = jnp.exp(
        jnp.arange(half_dim, dtype=jnp.float32) * (-2.0 * math.log(10000.0) / HEAD_DIM)
    )
    angles = offset.astype(jnp.float32)[..., None] * inverse
    return (jnp.cos(angles), jnp.sin(angles))


def rotate(values, cosine, sine):
    half_dim = values.shape[-1] // 2
    front_half = values[..., :half_dim]
    back_half = values[..., half_dim:]
    cos_wide = cosine[..., None, :]
    sin_wide = sine[..., None, :]
    return jnp.concatenate(
        [
            front_half * cos_wide - back_half * sin_wide,
            back_half * cos_wide + front_half * sin_wide,
        ],
        axis=-1,
    )


def swiglu(gate_up):
    half_cols = gate_up.shape[-1] // 2
    return jax.nn.silu(gate_up[:, :half_cols]) * gate_up[:, half_cols:]


def adam_update(weight, first_moment, second_moment, gradient, factor, use_decay, rate):
    clipped = gradient * factor
    first_new = beta_one * first_moment + (1.0 - beta_one) * clipped
    second_new = beta_two * second_moment + (1.0 - beta_two) * clipped * clipped
    first_hat = first_new / (1.0 - beta_one**STEP)
    second_hat = second_new / (1.0 - beta_two**STEP)
    direction = first_hat / (jnp.sqrt(second_hat) + adam_eps) + use_decay * weight_decay * weight
    return (clipped, weight - rate * direction, first_new, second_new)


def contract_rows(left, right):
    return lax.dot_general(
        left, right, (((0,), (0,)), ((), ())), preferred_element_type=jnp.float32
    )


def contract_cols(left, right):
    return lax.dot_general(
        left, right, (((1,), (1,)), ((), ())), preferred_element_type=jnp.float32
    )


def per_device(
    tokens,
    cotangent,
    lengths,
    qkv_master,
    qkv_first,
    qkv_second,
    out_master,
    out_first,
    out_second,
    in_master,
    in_first,
    in_second,
    down_master,
    down_first,
    down_second,
    norm_gains,
    gain_first,
    gain_second,
):
    heads_local = HEADS // lax.axis_size("tensor")
    width_local = heads_local * HEAD_DIM
    ffn_local = FF // lax.axis_size("tensor")
    row_count = lengths.shape[0]
    all_rows = row_count * ROW
    score_scale = HEAD_DIM ** (-0.5)
    block_rows = min(512, ROW)
    block_count = ROW // block_rows
    w_qkv, w_out, w_in, w_down = (
        lax.all_gather(qkv_master.astype(jnp.bfloat16), "dp", axis=0, tiled=True),
        lax.all_gather(out_master.astype(jnp.bfloat16), "dp", axis=0, tiled=True),
        lax.all_gather(in_master.astype(jnp.bfloat16), "dp", axis=0, tiled=True),
        lax.all_gather(down_master.astype(jnp.bfloat16), "dp", axis=0, tiled=True),
    )
    w_qkv = w_qkv.reshape(D, 3 * width_local)
    w_in = w_in.reshape(D, 2 * ffn_local)
    segment, offset = row_layout(lengths)
    cosine, sine = rotary_tables(offset)
    gain_one = norm_gains[0]
    gain_two = norm_gains[1]
    inputs = tokens.astype(jnp.float32)
    normed = layer_norm(inputs, gain_one)
    gathered_one = lax.all_gather(normed.astype(jnp.bfloat16), "tensor", axis=0, tiled=True)
    projected = jnp.dot(gathered_one, w_qkv, preferred_element_type=jnp.float32)
    projected = projected.reshape(row_count, ROW, 3, heads_local, HEAD_DIM)
    queries = rotate(projected[:, :, 0], cosine, sine).astype(jnp.bfloat16)
    keys = rotate(projected[:, :, 1], cosine, sine).astype(jnp.bfloat16)
    values = projected[:, :, 2].astype(jnp.bfloat16)

    def score_block(query_block, key_row, segment_block, segment_row):
        scores = (
            jnp.einsum("qhd,khd->hqk", query_block, key_row, preferred_element_type=jnp.float32)
            * score_scale
        )
        allowed = segment_block[:, None] == segment_row[None, :]
        return jnp.where(allowed[None], scores, -1e30)

    def forward_row(pieces):
        query_row, key_row, value_row, segment_row = pieces

        def forward_block(block_parts):
            query_block, segment_block = block_parts
            masked = score_block(query_block, key_row, segment_block, segment_row)
            row_max = jnp.max(masked, axis=-1, keepdims=True)
            log_total = (
                jnp.log(jnp.sum(jnp.exp(masked - row_max), axis=-1, keepdims=True)) + row_max
            )
            weights = jnp.exp(masked - log_total).astype(jnp.bfloat16)
            mixed_heads = jnp.einsum(
                "hqk,khd->qhd", weights, value_row, preferred_element_type=jnp.float32
            )
            return (mixed_heads.astype(jnp.bfloat16), log_total)

        return lax.map(
            forward_block,
            (
                query_row.reshape(block_count, block_rows, heads_local, HEAD_DIM),
                segment_row.reshape(block_count, block_rows),
            ),
        )

    mixed_heads, log_totals = lax.map(forward_row, (queries, keys, values, segment))
    attended = mixed_heads.reshape(all_rows, width_local)
    middle = inputs + lax.psum_scatter(
        jnp.dot(attended, w_out, preferred_element_type=jnp.float32),
        "tensor",
        scatter_dimension=0,
        tiled=True,
    )
    normed_two = layer_norm(middle, gain_two)
    gathered_two = lax.all_gather(normed_two.astype(jnp.bfloat16), "tensor", axis=0, tiled=True)
    gate_up = jnp.dot(gathered_two, w_in, preferred_element_type=jnp.float32)
    hidden = swiglu(gate_up).astype(jnp.bfloat16)
    output = middle + lax.psum_scatter(
        jnp.dot(hidden, w_down, preferred_element_type=jnp.float32).astype(jnp.bfloat16),
        "tensor",
        scatter_dimension=0,
        tiled=True,
    ).astype(jnp.float32)
    layer_out = output.astype(jnp.bfloat16)
    upstream = cotangent.astype(jnp.float32)
    gathered_down = lax.all_gather(cotangent, "tensor", axis=0, tiled=True)
    grad_down = contract_rows(hidden, gathered_down)
    hidden_grad = contract_cols(gathered_down, w_down)
    gate_up_grad = jax.vjp(swiglu, gate_up)[1](hidden_grad)[0].astype(jnp.bfloat16)
    grad_in = contract_rows(gathered_two, gate_up_grad)
    normed_two_grad = lax.psum_scatter(
        contract_cols(gate_up_grad, w_in).astype(jnp.bfloat16),
        "tensor",
        scatter_dimension=0,
        tiled=True,
    ).astype(jnp.float32)
    middle_back, gain_two_grad = jax.vjp(layer_norm, middle, gain_two)[1](normed_two_grad)
    middle_grad = upstream + middle_back
    gathered_mid = lax.all_gather(middle_grad.astype(jnp.bfloat16), "tensor", axis=0, tiled=True)
    grad_out = contract_rows(attended, gathered_mid)
    attended_grad = contract_cols(gathered_mid, w_out).astype(jnp.bfloat16)
    attended_grad = attended_grad.reshape(row_count, ROW, heads_local, HEAD_DIM)

    def backward_row(pieces):
        query_row, key_row, value_row, segment_row, total_row, grad_row = pieces

        def backward_block(running, block_parts):
            key_acc, value_acc = running
            query_block, segment_block, total_block, grad_block = block_parts
            masked = score_block(query_block, key_row, segment_block, segment_row)
            probs_block = jnp.exp(masked - total_block)
            probs_low = probs_block.astype(jnp.bfloat16)
            prob_grad = jnp.einsum(
                "qhd,khd->hqk", grad_block, value_row, preferred_element_type=jnp.float32
            )
            row_inner = jnp.sum(probs_block * prob_grad, axis=-1, keepdims=True)
            score_grad = (probs_block * (prob_grad - row_inner)).astype(jnp.bfloat16)
            query_grad = (
                jnp.einsum("hqk,khd->qhd", score_grad, key_row, preferred_element_type=jnp.float32)
                * score_scale
            )
            key_acc = (
                key_acc
                + jnp.einsum(
                    "hqk,qhd->khd", score_grad, query_block, preferred_element_type=jnp.float32
                )
                * score_scale
            )
            value_acc = value_acc + jnp.einsum(
                "hqk,qhd->khd", probs_low, grad_block, preferred_element_type=jnp.float32
            )
            return ((key_acc, value_acc), query_grad)

        zeros_acc = jnp.zeros((ROW, heads_local, HEAD_DIM), jnp.float32)
        block_inputs = (
            query_row.reshape(block_count, block_rows, heads_local, HEAD_DIM),
            segment_row.reshape(block_count, block_rows),
            total_row,
            grad_row.reshape(block_count, block_rows, heads_local, HEAD_DIM),
        )
        (key_grad, value_grad), query_grad = lax.scan(
            backward_block, (zeros_acc, zeros_acc), block_inputs
        )
        return (query_grad.reshape(ROW, heads_local, HEAD_DIM), key_grad, value_grad)

    query_grad, key_grad, value_grad = lax.map(
        backward_row, (queries, keys, values, segment, log_totals, attended_grad)
    )
    rotate_back = jax.vjp(partial(rotate, cosine=cosine, sine=sine), projected[:, :, 0])[1]
    query_raw = rotate_back(query_grad)[0]
    key_raw = rotate_back(key_grad)[0]
    qkv_grad_low = (
        jnp.stack([query_raw, key_raw, value_grad], axis=2)
        .reshape(all_rows, 3 * width_local)
        .astype(jnp.bfloat16)
    )
    grad_qkv = contract_rows(gathered_one, qkv_grad_low)
    normed_grad = lax.psum_scatter(
        contract_cols(qkv_grad_low, w_qkv).astype(jnp.bfloat16),
        "tensor",
        scatter_dimension=0,
        tiled=True,
    ).astype(jnp.float32)
    input_back, gain_one_grad = jax.vjp(layer_norm, inputs, gain_one)[1](normed_grad)
    input_grad = middle_grad + input_back
    reduced_qkv, reduced_out, reduced_in, reduced_down = (
        lax.psum_scatter(
            grad_qkv.reshape(D, 3, width_local).astype(jnp.bfloat16),
            "dp",
            scatter_dimension=0,
            tiled=True,
        ).astype(jnp.float32),
        lax.psum_scatter(
            grad_out.astype(jnp.bfloat16), "dp", scatter_dimension=0, tiled=True
        ).astype(jnp.float32),
        lax.psum_scatter(
            grad_in.reshape(D, 2, ffn_local).astype(jnp.bfloat16),
            "dp",
            scatter_dimension=0,
            tiled=True,
        ).astype(jnp.float32),
        lax.psum_scatter(
            grad_down.astype(jnp.bfloat16), "dp", scatter_dimension=0, tiled=True
        ).astype(jnp.float32),
    )
    local_squares = (
        jnp.sum(reduced_qkv * reduced_qkv)
        + jnp.sum(reduced_out * reduced_out)
        + jnp.sum(reduced_in * reduced_in)
        + jnp.sum(reduced_down * reduced_down)
    )
    gain_part = jnp.stack([gain_one_grad, gain_two_grad])
    gain_total, weight_squares = lax.psum((gain_part, local_squares), ("dp", "tensor"))
    grad_norm = jnp.sqrt(weight_squares + jnp.sum(gain_total * gain_total))
    factor = max_norm / jnp.maximum(grad_norm, max_norm)
    qkv_res = adam_update(qkv_master, qkv_first, qkv_second, reduced_qkv, factor, 1.0, learn_rate)
    out_res = adam_update(out_master, out_first, out_second, reduced_out, factor, 1.0, learn_rate)
    in_res = adam_update(in_master, in_first, in_second, reduced_in, factor, 1.0, learn_rate)
    down_res = adam_update(
        down_master, down_first, down_second, reduced_down, factor, 1.0, learn_rate
    )
    gain_res = adam_update(norm_gains, gain_first, gain_second, gain_total, factor, 0.0, gain_rate)
    return (
        layer_out,
        input_grad,
        qkv_res[0],
        qkv_res[1],
        qkv_res[2],
        qkv_res[3],
        out_res[0],
        out_res[1],
        out_res[2],
        out_res[3],
        in_res[0],
        in_res[1],
        in_res[2],
        in_res[3],
        down_res[0],
        down_res[1],
        down_res[2],
        down_res[3],
        gain_res[0],
        gain_res[1],
        gain_res[2],
        gain_res[3],
        grad_norm,
    )


def solution(mesh):
    placed = (
        P(("dp", "tensor"), None),
        P(("dp", "tensor"), None),
        P("dp", None),
        P("dp", None, "tensor"),
        P("dp", None, "tensor"),
        P("dp", None, "tensor"),
        P(("tensor", "dp"), None),
        P(("tensor", "dp"), None),
        P(("tensor", "dp"), None),
        P("dp", None, "tensor"),
        P("dp", None, "tensor"),
        P("dp", None, "tensor"),
        P(("tensor", "dp"), None),
        P(("tensor", "dp"), None),
        P(("tensor", "dp"), None),
        P(),
        P(),
        P(),
    )
    return jax.shard_map(
        per_device,
        mesh=mesh,
        in_specs=placed,
        out_specs=(
            P(("dp", "tensor"), None),
            P(("dp", "tensor"), None),
            P("dp", None, "tensor"),
            P("dp", None, "tensor"),
            P("dp", None, "tensor"),
            P("dp", None, "tensor"),
            P(("tensor", "dp"), None),
            P(("tensor", "dp"), None),
            P(("tensor", "dp"), None),
            P(("tensor", "dp"), None),
            P("dp", None, "tensor"),
            P("dp", None, "tensor"),
            P("dp", None, "tensor"),
            P("dp", None, "tensor"),
            P(("tensor", "dp"), None),
            P(("tensor", "dp"), None),
            P(("tensor", "dp"), None),
            P(("tensor", "dp"), None),
            P(),
            P(),
            P(),
            P(),
            P(),
        ),
        check_vma=False,
    )
```

profile of v0, /device:TPU:0, one launch (start us, length us, event | category | flops | bytes accessed | tf_op | source)
XLA Modules:
  0.0 1104.2 jit_solution(1875028781626215786)
XLA Ops:
  16.8 36.3 %all_gather.26 = bf16[256,1024]{1,0:T(8,128)(2,1)} all-gather(bf16[32,1024]{1,0:T(8,128)(2,1)S(1)} %convert_element_type.159), channel_id=1, replica_groups=mesh['dp'=8,'tensor'=4] {'dp'}, dimensions={0}, use_global_device_ids=true | all-gather | bytes 589824 | tf_op jit(solution)/shard_map/all_gather | solution.py:123
  54.1 7.5 all-gather.10.cloned.1.call-done
  61.6 35.9 %all-gather.8.cloned.1.call-done = bf16[2048,1024]{1,0:T(8,128)(2,1)} async-done(((bf16[512,1024]{1,0:T(8,128)(2,1)}), bf16[2048,1024]{1,0:T(8,128)(2,1)}) %all-gather.8.cloned.1.call-update) | async-done | bytes 4194320 | tf_op jit(solution)/shard_map/all_gather | solution.py:135
  97.5 5.9 fusion.48
  109.8 57.2 %while.47 = (s32[]{:T(128)}, bf16[4,512,4,64]{1,3,2,0:T(8,128)(2,1)}, f32[4,4,512,1]{2,1,3,0:T(4,128)}, s32[4,512]{1,0:T(4,128)S(1)}, s32[2048]{0:T(1024)S(1)}, ...) while((s32[]{:T(128)}, ...), condition=%wide.region_8.9_spmd, body=%wide.region_5.8_spmd.sunk | while | flops 1121056768 | bytes 57227380 | solution.py:166
  132.9 5.5 fusion.144
  178.1 69.5 %reduce-scatter.8.cloned.1.call-done = f32[512,1024]{1,0:T(8,128)} async-done(((f32[2048,1024]{1,0:T(8,128)}), f32[512,1024]{1,0:T(8,128)}) %reduce-scatter.8.cloned.1.call-update) | async-done | bytes 2097168 | tf_op jit(solution)/shard_map/reduce_scatter | solution.py:176
  254.0 69.7 %all-gather.14.cloned.1.call-done = bf16[1024,2,1024]{2,1,0:T(2,128)(2,1)} async-done(((bf16[128,2,1024]{2,1,0:T(2,128)(2,1)}), bf16[1024,2,1024]{2,1,0:T(2,128)(2,1)}) %all-gather.14.cloned.1.call-update) | async-done | bytes 4194320 | tf_op jit(solution)/shard_map/all_gather | solution.py:124
  323.8 5.6 copy.103
  329.4 29.2 %all-gather.12.cloned.1.call-done = bf16[2048,1024]{1,0:T(8,128)(2,1)} async-done(((bf16[512,1024]{1,0:T(8,128)(2,1)}), bf16[2048,1024]{1,0:T(8,128)(2,1)}) %all-gather.12.cloned.1.call-update) | async-done | bytes 4194320 | tf_op jit(solution)/shard_map/all_gather | solution.py:183
  358.6 15.1 %fusion.96 = f32[2048,2048]{1,0:T(8,128)} fusion(bf16[2048,1024]{1,0:T(8,128)(2,1)} %all-gather.12.cloned.1.call-done, bf16[1024,2048]{1,0:T(8,128)(2,1)} %bitcast.176), kind=kOutput, calls=%fused_computation.180 | convolution fusion | flops 8589934592 | bytes 25165824 | tf_op jit(solution)/shard_map/dot_general | solution.py:184
  373.7 37.0 %all-gather.16.cloned.1.call-done = bf16[1024,1024]{1,0:T(8,128)(2,1)} async-done(((bf16[128,1024]{1,0:T(8,128)(2,1)}), bf16[1024,1024]{1,0:T(8,128)(2,1)}) %all-gather.16.cloned.1.call-update) | async-done | bytes 2097168 | tf_op jit(solution)/shard_map/all_gather | solution.py:125
  410.7 34.6 %all-gather.18.cloned.1.call-done = bf16[2048,1024]{1,0:T(8,128)(2,1)} async-done(((bf16[512,1024]{1,0:T(8,128)(2,1)}), bf16[2048,1024]{1,0:T(8,128)(2,1)}) %all-gather.18.cloned.1.call-update) | async-done | bytes 4194320 | tf_op jit(solution)/shard_map/all_gather | solution.py:194
  445.3 17.2 %fusion.73 = (f32[2048,1024]{1,0:T(8,128)}, f32[2048,1024]{1,0:T(8,128)}, bf16[2048,1024]{1,0:T(8,128)(2,1)}) fusion(f32[2048,2048]{1,0:T(8,128)} %fusion.96, bf16[2048,1024]{1,0:T(8,128)(2,1)} %all-gather.18.cloned.1.call-done, bf16[1024,1024]{1,0:T(8,128)(2,1)} %all-gather.16.cloned.1.call-done), kind=kOutput, calls=%fused_computation.124 | convolution fusion | flops 4324327424 | bytes 44040192 | tf_op jit(solution)/shard_map/dot_general | solution.py:88
  462.5 15.1 %convolution_convert_fusion.1 = bf16[2048,1024]{1,0:T(8,128)(2,1)} fusion(bf16[1024,2048]{1,0:T(8,128)(2,1)} %bitcast.177, f32[2048,1024]{1,0:T(8,128)} %get-tuple-element.338, f32[2048,1024]{1,0:T(8,128)} %get-tuple-element.337), kind=kOutput, calls=%fused_computation.65 | convolution fusion | flops 8600420352 | bytes 25165824 | tf_op jit(solution)/shard_map/dot_general | solution.py:88
  477.8 9.7 convolution_convert_fusion.3
  487.6 34.7 %reduce-scatter.12.cloned.1.call-done = bf16[512,1024]{1,0:T(8,128)(2,1)} async-done(((bf16[2048,1024]{1,0:T(8,128)(2,1)}), bf16[512,1024]{1,0:T(8,128)(2,1)}) %reduce-scatter.12.cloned.1.call-update) | async-done | bytes 1048592 | tf_op jit(solution)/shard_map/reduce_scatter | solution.py:199
  524.9 44.4 %reduce-scatter.10.cloned.1.call-done = bf16[512,1024]{1,0:T(8,128)(2,1)} async-done(((bf16[2048,1024]{1,0:T(8,128)(2,1)}), bf16[512,1024]{1,0:T(8,128)(2,1)}) %reduce-scatter.10.cloned.1.call-update) | async-done | bytes 1048592 | tf_op jit(solution)/shard_map/reduce_scatter | solution.py:186
  575.4 17.0 %convolution_convert_fusion = bf16[1024,2048]{1,0:T(8,128)(2,1)} fusion(bf16[2048,1024]{1,0:T(8,128)(2,1)} %all-gather.12.cloned.1.call-done, f32[2048,1024]{1,0:T(8,128)} %get-tuple-element.338, f32[2048,1024]{1,0:T(8,128)} %get-tuple-element.337), kind=kOutput, calls=%fused_computation.64 | convolution fusion | flops 8600420352 | bytes 25165824 | tf_op jit(solution)/shard_map/dot_general | solution.py:82
  592.4 7.9 convert_element_type.182
  600.4 9.4 convolution_convert_fusion.5
  620.1 230.4 %while.48 = (s32[]{:T(128)}, f32[2048,4,64]{0,2,1:T(8,128)}, f32[2048,4,64]{0,2,1:T(8,128)}, f32[4,512,4,64]{1,0,3,2:T(4,128)}, bf16[4,512,4,64]{1,3,2,0:T(8,128...) while((s32[]{:T(128)}, f32[2048,4,64]{0,2,1:T(8,128)}, ...), condition=%wide.region_18.19_spmd.clone, body=%wide.region_16.18_spmd.clone.sunk | while | flops 2751068160 | bytes 183179600 | solution.py:249
  625.5 7.2 fusion.156
  632.7 11.5 %multiply_reduce_fusion.4 = (f32[4,512]{1,0:T(4,128)}, f32[4,512,2048]{2,1,0:T(8,128)}) fusion(f32[4,512,2048]{2,1,0:T(8,128)S(1)} %fusion.154, f32[4,512]{1,0:T(4,128)S(1)} %dynamic-slice_bitcast_fusion.2, pred[512,2048]{1,0:T(8,128)(4,1)} %copy-done.1, bf16[2048,4,64]{0,2,1:T(8,128)(2,1)} %get-tuple-element.552, ...), kind=kOutput, calls=%fused_computation.20.clone.1 | convolution fusion | flops 557840384 | bytes 35930116 | tf_op jit(solution)/shard_map/while/body/eval_jaxpr/while/body/eval_jaxpr/qhd,khd->hqk/dot_general | solution.py:221
  644.2 11.1 %multiply_convert_fusion.4 = bf16[4,512,2048]{2,1,0:T(8,128)(2,1)} fusion(f32[4,512,2048]{2,1,0:T(8,128)} %get-tuple-element.487, f32[4,512,2048]{2,1,0:T(8,128)S(1)} %fusion.154, f32[4,512]{1,0:T(4,128)} %get-tuple-element.488, f32[4,512]{1,0:T(4,128)S(1)} %dynamic-slice_bitcast_fusion.2, pred[512,2048]{1,0:T(8,128)(4,1)} %copy-done.1), kind=kLoop, calls=%fused_computation.19.clone.1 | loop fusion | flops 25165824 | bytes 43008000 | tf_op jit(solution)/shard_map/while/body/eval_jaxpr/while/body/eval_jaxpr/convert_element_type | solution.py:225
  655.4 6.2 fusion.157
  666.1 11.1 %dynamic_update_slice.33 = f32[4,512,4,64]{1,0,3,2:T(4,128)} dynamic-update-slice(f32[4,512,4,64]{1,0,3,2:T(4,128)} %get-tuple-element.532, f32[1,512,4,64]{1,0,3,2:T(1,128)S(1)} %copy.107, s32[]{:T(128)S(6)} %copy.125, s32[]{:T(128)} %constant.79.clone.1..sunk, s32[]{:T(128)} %constant.79.clone.1..sunk, s32[]{:T(128)} %constant.79.clone.1..sunk) | dynamic-update-slice | bytes 1048580 | tf_op jit(solution)/shard_map/while/body/eval_jaxpr/while/body/jit(dynamic_update_index_in_dim)/dynamic_update_slice | solution.py:249
  682.1 7.6 fusion.156
  689.8 11.5 %multiply_reduce_fusion.4 = (f32[4,512]{1,0:T(4,128)}, f32[4,512,2048]{2,1,0:T(8,128)}) fusion(f32[4,512,2048]{2,1,0:T(8,128)S(1)} %fusion.154, f32[4,512]{1,0:T(4,128)S(1)} %dynamic-slice_bitcast_fusion.2, pred[512,2048]{1,0:T(8,128)(4,1)} %copy-done.1, bf16[2048,4,64]{0,2,1:T(8,128)(2,1)} %get-tuple-element.552, ...), kind=kOutput, calls=%fused_computation.20.clone.1 | convolution fusion | flops 557840384 | bytes 35930116 | tf_op jit(solution)/shard_map/while/body/eval_jaxpr/while/body/eval_jaxpr/qhd,khd->hqk/dot_general | solution.py:221
  701.3 11.0 %multiply_convert_fusion.4 = bf16[4,512,2048]{2,1,0:T(8,128)(2,1)} fusion(f32[4,512,2048]{2,1,0:T(8,128)} %get-tuple-element.487, f32[4,512,2048]{2,1,0:T(8,128)S(1)} %fusion.154, f32[4,512]{1,0:T(4,128)} %get-tuple-element.488, f32[4,512]{1,0:T(4,128)S(1)} %dynamic-slice_bitcast_fusion.2, pred[512,2048]{1,0:T(8,128)(4,1)} %copy-done.1), kind=kLoop, calls=%fused_computation.19.clone.1 | loop fusion | flops 25165824 | bytes 43008000 | tf_op jit(solution)/shard_map/while/body/eval_jaxpr/while/body/eval_jaxpr/convert_element_type | solution.py:225
  712.3 6.2 fusion.157
  723.9 11.1 %dynamic_update_slice.33 = f32[4,512,4,64]{1,0,3,2:T(4,128)} dynamic-update-slice(f32[4,512,4,64]{1,0,3,2:T(4,128)} %get-tuple-element.532, f32[1,512,4,64]{1,0,3,2:T(1,128)S(1)} %copy.107, s32[]{:T(128)S(6)} %copy.125, s32[]{:T(128)} %constant.79.clone.1..sunk, s32[]{:T(128)} %constant.79.clone.1..sunk, s32[]{:T(128)} %constant.79.clone.1..sunk) | dynamic-update-slice | bytes 1048580 | tf_op jit(solution)/shard_map/while/body/eval_jaxpr/while/body/jit(dynamic_update_index_in_dim)/dynamic_update_slice | solution.py:249
  739.9 7.6 fusion.156
  747.6 11.5 %multiply_reduce_fusion.4 = (f32[4,512]{1,0:T(4,128)}, f32[4,512,2048]{2,1,0:T(8,128)}) fusion(f32[4,512,2048]{2,1,0:T(8,128)S(1)} %fusion.154, f32[4,512]{1,0:T(4,128)S(1)} %dynamic-slice_bitcast_fusion.2, pred[512,2048]{1,0:T(8,128)(4,1)} %copy-done.1, bf16[2048,4,64]{0,2,1:T(8,128)(2,1)} %get-tuple-element.552, ...), kind=kOutput, calls=%fused_computation.20.clone.1 | convolution fusion | flops 557840384 | bytes 35930116 | tf_op jit(solution)/shard_map/while/body/eval_jaxpr/while/body/eval_jaxpr/qhd,khd->hqk/dot_general | solution.py:221
  759.1 11.0 multiply_convert_fusion.4
  770.1 6.2 fusion.157
  781.5 11.1 %dynamic_update_slice.33 = f32[4,512,4,64]{1,0,3,2:T(4,128)} dynamic-update-slice(f32[4,512,4,64]{1,0,3,2:T(4,128)} %get-tuple-element.532, f32[1,512,4,64]{1,0,3,2:T(1,128)S(1)} %copy.107, s32[]{:T(128)S(6)} %copy.125, s32[]{:T(128)} %constant.79.clone.1..sunk, s32[]{:T(128)} %constant.79.clone.1..sunk, s32[]{:T(128)} %constant.79.clone.1..sunk) | dynamic-update-slice | bytes 1048580 | tf_op jit(solution)/shard_map/while/body/eval_jaxpr/while/body/jit(dynamic_update_index_in_dim)/dynamic_update_slice | solution.py:249
  797.6 7.6 fusion.156
  805.2 11.6 %multiply_reduce_fusion.4 = (f32[4,512]{1,0:T(4,128)}, f32[4,512,2048]{2,1,0:T(8,128)}) fusion(f32[4,512,2048]{2,1,0:T(8,128)S(1)} %fusion.154, f32[4,512]{1,0:T(4,128)S(1)} %dynamic-slice_bitcast_fusion.2, pred[512,2048]{1,0:T(8,128)(4,1)} %copy-done.1, bf16[2048,4,64]{0,2,1:T(8,128)(2,1)} %get-tuple-element.552, ...), kind=kOutput, calls=%fused_computation.20.clone.1 | convolution fusion | flops 557840384 | bytes 35930116 | tf_op jit(solution)/shard_map/while/body/eval_jaxpr/while/body/eval_jaxpr/qhd,khd->hqk/dot_general | solution.py:221
  816.8 11.0 multiply_convert_fusion.4
  827.8 6.2 fusion.157
  839.3 11.1 %dynamic_update_slice.33 = f32[4,512,4,64]{1,0,3,2:T(4,128)} dynamic-update-slice(f32[4,512,4,64]{1,0,3,2:T(4,128)} %get-tuple-element.532, f32[1,512,4,64]{1,0,3,2:T(1,128)S(1)} %copy.107, s32[]{:T(128)S(6)} %copy.125, s32[]{:T(128)} %constant.79.clone.1..sunk, s32[]{:T(128)} %constant.79.clone.1..sunk, s32[]{:T(128)} %constant.79.clone.1..sunk) | dynamic-update-slice | bytes 1048580 | tf_op jit(solution)/shard_map/while/body/eval_jaxpr/while/body/jit(dynamic_update_index_in_dim)/dynamic_update_slice | solution.py:249
  870.1 7.0 convolution_convert_fusion.2
  883.5 37.4 %reduce-scatter.18.cloned.1.call-done = bf16[32,1024]{1,0:T(8,128)(2,1)} async-done(((bf16[256,1024]{1,0:T(8,128)(2,1)}), bf16[32,1024]{1,0:T(8,128)(2,1)}) %reduce-scatter.18.cloned.1.call-update) | async-done | bytes 65552 | tf_op jit(solution)/shard_map/reduce_scatter | solution.py:281
  922.3 67.0 %reduce-scatter.16.cloned.1.call-done = bf16[128,3,256]{2,0,1:T(8,128)(2,1)} async-done(((bf16[1024,3,256]{2,0,1:T(8,128)(2,1)}), bf16[128,3,256]{2,0,1:T(8,128)(2,1)}) %reduce-scatter.16.cloned.1.call-update) | async-done | bytes 196624 | tf_op jit(solution)/shard_map/reduce_scatter | solution.py:275
  993.5 41.8 %reduce-scatter.14.cloned.1.call-done = bf16[512,1024]{1,0:T(8,128)(2,1)} async-done(((bf16[2048,1024]{1,0:T(8,128)(2,1)}), bf16[512,1024]{1,0:T(8,128)(2,1)}) %reduce-scatter.14.cloned.1.call-update) | async-done | bytes 1048592 | tf_op jit(solution)/shard_map/reduce_scatter | solution.py:266
  1039.6 39.7 %all-reduce.7 = (f32[]{:T(128)}, f32[2,1024]{1,0:T(2,128)S(1)}) all-reduce(f32[]{:T(128)S(6)} %add.210, f32[2,1024]{1,0:T(2,128)S(1)} %pad_maximum_fusion.1), channel_id=1, replica_groups=mesh['dp'=8,'tensor'=4] {'dp','tensor'}, use_global_device_ids=true, to_apply=%region_30.31 | all-reduce | flops 2049 | bytes 16392 | tf_op jit(solution)/shard_map/psum | solution.py:301
  1086.2 6.5 multiply_subtract_fusion
  (297 shorter events, 186.3 us)
Async XLA Ops:
  7.2 9.1 copy-start.52
  7.2 9.6 copy-start.29
  7.2 54.4 %all-gather.10.cloned.1.call-start = ((), (), s32[]{:S(2)}) async-start(), calls=%async_computation.8 | async-start | bytes 1769472 | tf_op jit(solution)/shard_map/all_gather | solution.py:122
  9.1 88.4 %all-gather.8.cloned.1.call-start = ((), (), s32[]{:S(2)}) async-start(), calls=%async_computation.7 | async-start | bytes 5242880 | tf_op jit(solution)/shard_map/all_gather | solution.py:135
  16.3 231.3 %reduce-scatter.8.cloned.1.call-start = ((), (), s32[]{:S(2)}) async-start(), calls=%async_computation.9 | async-start | bytes 10485760 | tf_op jit(solution)/shard_map/reduce_scatter | solution.py:176
  54.1 50.0 %copy-start.14 = (f32[2048,32]{0,1:T(8,128)}, f32[2048,32]{0,1:T(8,128)S(1)}, u32[]{:S(2)}) copy-start(f32[2048,32]{0,1:T(8,128)S(1)} %get-tuple-element.355) | copy-start | bytes 786436
  54.1 50.0 %copy-start.16 = (f32[2048,32]{0,1:T(8,128)}, f32[2048,32]{0,1:T(8,128)S(1)}, u32[]{:S(2)}) copy-start(f32[2048,32]{0,1:T(8,128)S(1)} %get-tuple-element.356) | copy-start | bytes 786436
  167.0 8.6 copy-start.4
  167.0 8.6 copy-start.5
  175.6 148.1 %all-gather.14.cloned.1.call-start = ((), (), s32[]{:S(2)}) async-start(), calls=%async_computation.11 | async-start | bytes 4718592 | tf_op jit(solution)/shard_map/all_gather | solution.py:124
  178.0 180.6 %all-gather.12.cloned.1.call-start = ((), (), s32[]{:S(2)}) async-start(), calls=%async_computation.10 | async-start | bytes 5242880 | tf_op jit(solution)/shard_map/all_gather | solution.py:183
  251.4 159.3 %all-gather.16.cloned.1.call-start = ((), (), s32[]{:S(2)}) async-start(), calls=%async_computation.12 | async-start | bytes 2359296 | tf_op jit(solution)/shard_map/all_gather | solution.py:125
  253.2 192.1 %all-gather.18.cloned.1.call-start = ((), (), s32[]{:S(2)}) async-start(), calls=%async_computation.14 | async-start | bytes 5242880 | tf_op jit(solution)/shard_map/all_gather | solution.py:194
  254.0 268.3 %reduce-scatter.12.cloned.1.call-start = ((), (), s32[]{:S(2)}) async-start(), calls=%async_computation.15 | async-start | bytes 5242880 | tf_op jit(solution)/shard_map/reduce_scatter | solution.py:199
  477.6 91.7 %reduce-scatter.10.cloned.1.call-start = ((), (), s32[]{:S(2)}) async-start(), calls=%async_computation.13 | async-start | bytes 5242880 | tf_op jit(solution)/shard_map/reduce_scatter | solution.py:186
  487.5 122.5 %all-gather.20.cloned.1.call-start = ((), (), s32[]{:S(2)}) async-start(), calls=%async_computation.16 | async-start | bytes 5242880 | tf_op jit(solution)/shard_map/all_gather | solution.py:207
  572.8 19.7 %copy-start.45 = (f32[512]{0:T(512)}, f32[512]{0:T(512)S(1)}, u32[]{:S(2)}) copy-start(f32[512]{0:T(512)S(1)} %negate_multiply_fusion.1) | copy-start | bytes 6148
  575.4 303.7 %all-reduce.10.cloned.1.call-start = ((), (), s32[]{:S(2)}) async-start(), calls=%async_computation.21 | async-start | bytes 8388608
  600.3 281.4 %reduce-scatter.20.cloned.1.call-start = ((), (), s32[]{:S(2)}) async-start(), calls=%async_computation.20 | async-start | bytes 2359296 | tf_op jit(solution)/shard_map/reduce_scatter | solution.py:290
  600.4 9.6 copy-start.19
  609.9 311.0 %reduce-scatter.18.cloned.1.call-start = ((), (), s32[]{:S(2)}) async-start(), calls=%async_computation.19 | async-start | bytes 589824 | tf_op jit(solution)/shard_map/reduce_scatter | solution.py:281
  661.6 15.6 %copy-start.22 = (s32[2048]{0:T(1024)S(1)}, s32[2048]{0:T(1024)}, u32[]{:S(2)}) copy-start(s32[2048]{0:T(1024)} %copy-done.21) | copy-start | bytes 24580 | tf_op jit(solution)/shard_map/while/body/eval_jaxpr/while
  661.6 15.6 %copy-start.39 = (s32[4,512]{1,0:T(4,128)S(1)}, s32[4,512]{1,0:T(4,128)}, u32[]{:S(2)}) copy-start(s32[4,512]{1,0:T(4,128)} %copy-done.38) | copy-start | bytes 24580 | tf_op jit(solution)/shard_map/while/body/eval_jaxpr/while
  718.5 16.4 %copy-start.22 = (s32[2048]{0:T(1024)S(1)}, s32[2048]{0:T(1024)}, u32[]{:S(2)}) copy-start(s32[2048]{0:T(1024)} %copy-done.21) | copy-start | bytes 24580 | tf_op jit(solution)/shard_map/while/body/eval_jaxpr/while
  718.6 16.4 %copy-start.39 = (s32[4,512]{1,0:T(4,128)S(1)}, s32[4,512]{1,0:T(4,128)}, u32[]{:S(2)}) copy-start(s32[4,512]{1,0:T(4,128)} %copy-done.38) | copy-start | bytes 24580 | tf_op jit(solution)/shard_map/while/body/eval_jaxpr/while
  776.3 16.3 %copy-start.22 = (s32[2048]{0:T(1024)S(1)}, s32[2048]{0:T(1024)}, u32[]{:S(2)}) copy-start(s32[2048]{0:T(1024)} %copy-done.21) | copy-start | bytes 24580 | tf_op jit(solution)/shard_map/while/body/eval_jaxpr/while
  776.3 16.3 %copy-start.39 = (s32[4,512]{1,0:T(4,128)S(1)}, s32[4,512]{1,0:T(4,128)}, u32[]{:S(2)}) copy-start(s32[4,512]{1,0:T(4,128)} %copy-done.38) | copy-start | bytes 24580 | tf_op jit(solution)/shard_map/while/body/eval_jaxpr/while
  834.0 16.3 %copy-start.22 = (s32[2048]{0:T(1024)S(1)}, s32[2048]{0:T(1024)}, u32[]{:S(2)}) copy-start(s32[2048]{0:T(1024)} %copy-done.21) | copy-start | bytes 24580 | tf_op jit(solution)/shard_map/while/body/eval_jaxpr/while
  834.0 16.3 %copy-start.39 = (s32[4,512]{1,0:T(4,128)S(1)}, s32[4,512]{1,0:T(4,128)}, u32[]{:S(2)}) copy-start(s32[4,512]{1,0:T(4,128)} %copy-done.38) | copy-start | bytes 24580 | tf_op jit(solution)/shard_map/while/body/eval_jaxpr/while
  858.7 130.6 %reduce-scatter.16.cloned.1.call-start = ((), (), s32[]{:S(2)}) async-start(), calls=%async_computation.18 | async-start | bytes 1769472 | tf_op jit(solution)/shard_map/reduce_scatter | solution.py:275
  870.0 165.3 %reduce-scatter.14.cloned.1.call-start = ((), (), s32[]{:S(2)}) async-start(), calls=%async_computation.17 | async-start | bytes 5242880 | tf_op jit(solution)/shard_map/reduce_scatter | solution.py:266
  877.1 158.2 %copy-start.3 = (bf16[512,1024]{1,0:T(8,128)(2,1)S(1)}, bf16[512,1024]{1,0:T(8,128)(2,1)}, u32[]{:S(2)}) copy-start(bf16[512,1024]{1,0:T(8,128)(2,1)} %param.22) | copy-start | bytes 3145732
  877.1 158.2 %copy-start.37 = (f32[1,1024]{1,0:T(1,128)S(1)}, f32[1,1024]{1,0:T(1,128)}, u32[]{:S(2)}) copy-start(f32[1,1024]{1,0:T(1,128)} %copy-done.36) | copy-start | bytes 12292
  877.1 158.2 %copy-start.41 = (f32[512]{0:T(512)S(1)}, f32[512]{0:T(512)}, u32[]{:S(2)}) copy-start(f32[512]{0:T(512)} %copy-done.40) | copy-start | bytes 6148
  877.1 160.0 %copy-start.48 = (f32[512]{0:T(512)S(1)}, f32[512]{0:T(512)}, u32[]{:S(2)}) copy-start(f32[512]{0:T(512)} %copy-done.47) | copy-start | bytes 6148
  877.2 160.0 %copy-start.44 = (f32[512]{0:T(512)S(1)}, f32[512]{0:T(512)}, u32[]{:S(2)}) copy-start(f32[512]{0:T(512)} %copy-done.43) | copy-start | bytes 6148
  877.2 162.4 %copy-start.49 = (f32[1024]{0:T(1024)S(1)}, f32[1024]{0:T(1024)}, u32[]{:S(2)}) copy-start(f32[1024]{0:T(1024)} %get-tuple-element.261) | copy-start | bytes 12292
  877.2 204.1 %copy-start.42 = (f32[2,1024]{1,0:T(2,128)S(1)}, f32[2,1024]{1,0:T(2,128)}, u32[]{:S(2)}) copy-start(f32[2,1024]{1,0:T(2,128)} %param.37) | copy-start | bytes 24580
  877.2 204.1 %copy-start.50 = (f32[2,1024]{1,0:T(2,128)S(1)}, f32[2,1024]{1,0:T(2,128)}, u32[]{:S(2)}) copy-start(f32[2,1024]{1,0:T(2,128)} %param.38) | copy-start | bytes 24580
  877.2 204.1 %copy-start.51 = (f32[2,1024]{1,0:T(2,128)S(1)}, f32[2,1024]{1,0:T(2,128)}, u32[]{:S(2)}) copy-start(f32[2,1024]{1,0:T(2,128)} %param.39) | copy-start | bytes 24580
  877.2 204.8 %copy-start.7 = (f32[512,1024]{1,0:T(8,128)S(1)}, f32[512,1024]{1,0:T(8,128)}, u32[]{:S(2)}) copy-start(f32[512,1024]{1,0:T(8,128)} %copy-done.6) | copy-start | bytes 6291460
  877.2 204.8 %copy-start.46 = (f32[512]{0:T(512)S(1)}, f32[512]{0:T(512)}, u32[]{:S(2)}) copy-start(f32[512]{0:T(512)} %copy-done.45) | copy-start | bytes 6148
  1086.1 7.4 copy-start.20
  1086.1 7.4 copy-start.26
  1086.1 8.6 copy-start.17
  1086.1 8.6 copy-start.25
  1086.2 8.6 copy-start.27
  1086.2 8.6 copy-start.28
  (41 other events, 149.8 us)
Sparse Core Ops, SparseCore 0:
  10.7 50.9 all-gather.9
  63.8 33.7 all-gather.7
  175.8 71.7 reduce-scatter.7
  250.3 73.3 all-gather.13
  325.8 32.7 all-gather.11
  361.4 49.2 all-gather.15
  412.3 32.9 all-gather.17
  477.7 44.4 reduce-scatter.11
  524.8 44.4 reduce-scatter.9
  575.5 34.4 all-gather.19
  614.2 156.2 all-reduce.9
  774.3 66.6 reduce-scatter.19
  858.8 62.0 reduce-scatter.17
  924.7 64.5 reduce-scatter.15
  991.8 43.4 reduce-scatter.13
where the time goes:
time: 1110 us; the launch traced here: 1100 us
  waiting for transfers between devices  510 us (46%)
  matrix products  282 us (25%)
  other arithmetic  125 us (11%)
  local copies, waits for them, and re-layouts  88.2 us (8%)
  blocking collectives  76 us (7%)
  between operations  20.6 us (2%)
    all_gather x1, waiting for transfers between devices, per_device(): lax.all_gather(in_master.astype(jnp.bfloat16), 'dp', axis=0, tiled=True)  69.7 us
    reduce_scatter x1, waiting for transfers between devices, per_device(): lax.psum_scatter(jnp.dot(attended, w_out, preferred_element_type=jnp.floa...  69.5 us
    reduce_scatter x1, waiting for transfers between devices, per_device(): lax.psum_scatter(grad_qkv.reshape(D, 3, width_local).astype(jnp.bfloat16)...  67 us
    dynamic_update_slice x8, local copies, waits for them, and re-layouts, backward_row(): lax.scan(backward_block, (zeros_acc, zeros_acc), block_inputs)  46.6 us
    dot_general x4, matrix products, backward_block(): jnp.einsum('qhd,khd->hqk', grad_block, value_row, preferred_element_type=...  46.1 us
    reduce_scatter x1, waiting for transfers between devices, per_device(): lax.psum_scatter(jnp.dot(hidden, w_down, preferred_element_type=jnp.float...  44.4 us
    convert_element_type x4, other arithmetic, backward_block(): score_grad = (probs_block * (prob_grad - row_inner)).astype(jnp.bfloat16)  44.2 us
    dot_general x4, matrix products, contract_cols(): lax.dot_general(left, right, (((1,), (1,)), ((), ())), preferred_element_...  43.7 us
  transfers between devices with their start and end apart: 15, of which 13 were waited for; matrix products, arithmetic and copies ran while one was open for 32% of the time, Pallas kernels for 0%

commit v1 on v0

v1 whole, which is shorter than its diff:
```python
import functools
import math

import jax
import jax.numpy as jnp
from jax import lax
from jax.experimental import pallas as pl
from jax.experimental.pallas import tpu as pltpu
from jax.sharding import PartitionSpec as P

D = 1024
HEADS = 16
HEAD_DIM = 64
FF = 4096
ROW = 2048
STEP = 5
MOST = 256

eps_norm = 1e-05
beta_one = 0.9
beta_two = 0.999
learn_rate = 0.05
gain_rate = 0.6
weight_decay = 0.1
adam_eps = 1e-08
max_norm = 1.0

BF = jnp.bfloat16
F32 = jnp.float32
TP = 4
PIECE = ROW // TP
BLK = 256
SPAN = 3 * BLK
NB = ROW // BLK
HL = HEADS // TP
WL = HL * HEAD_DIM
FL = FF // TP
VMEM_LIMIT = 60 * 1024 * 1024

NT = (((1,), (1,)), ((), ()))
TN = (((0,), (0,)), ((), ()))
NN = (((1,), (0,)), ((), ()))


def mm(a, b, dims=NN):
    return lax.dot_general(a, b, dims, preferred_element_type=F32)


def layer_norm(values, gain):
    centre = values - jnp.mean(values, axis=-1, keepdims=True)
    spread = jnp.mean(centre * centre, axis=-1, keepdims=True)
    return centre * lax.rsqrt(spread + eps_norm) * gain


def swap(x, axis, k):
    return lax.ppermute(x, axis, [(i, i ^ k) for i in range(lax.axis_size(axis))])


def gather_pieces(own):
    near = swap(own, "tensor", 1)
    far = swap(own, "tensor", 2)
    return own, near, far, swap(far, "tensor", 1)


def scatter_sum(p0, p1, p2, p3):
    far = (p2.astype(F32) + swap(p3, "tensor", 1).astype(F32)).astype(BF)
    near = swap(p1, "tensor", 1)
    return p0.astype(F32) + near.astype(F32) + swap(far, "tensor", 2).astype(F32)


def rope_slab(u, cos, sin, lane_low):
    swapped = jnp.where(lane_low, pltpu.roll(u, 128 - 32, 1), pltpu.roll(u, 32, 1))
    return u * cos + swapped * sin


def head_mask(h, rows, dtype):
    lane = lax.broadcasted_iota(jnp.int32, (rows, WL), 1)
    return (lane // HEAD_DIM == h).astype(dtype)


def span_start(i):
    return pl.multiple_of(jnp.clip(i - 1, 0, NB - 3) * BLK, BLK)


def attn_fwd_body(t_ref, a0, a1, a2, a3, w_ref, wo_ref, cos_ref, sin_ref, segc_ref, segr_ref,
                  qkv_ref, o_ref, lse_ref, r0, r1, r2, r3):
    t = t_ref[0]
    low = lax.broadcasted_iota(jnp.int32, (BLK, 128), 1) % HEAD_DIM < HEAD_DIM // 2
    per = PIECE // BLK
    for j, a_ref in enumerate((a0, a1, a2, a3)):
        for half in range(per):
            row = pl.multiple_of((t ^ j) * PIECE + half * BLK, BLK)
            p = mm(a_ref[half * BLK:(half + 1) * BLK, :], w_ref[...])
            cos = cos_ref[pl.ds(row, BLK), :]
            sin = sin_ref[pl.ds(row, BLK), :]
            for s in range(2 * WL // 128):
                u = rope_slab(p[:, s * 128:(s + 1) * 128], cos, sin, low)
                if s < WL // 128:
                    u = u * (HEAD_DIM ** -0.5)
                qkv_ref[pl.ds(row, BLK), s * 128:(s + 1) * 128] = u.astype(BF)
            qkv_ref[pl.ds(row, BLK), 2 * WL:] = p[:, 2 * WL:].astype(BF)
    masks = [head_mask(h, BLK, BF) for h in range(HL)]
    masks_f = [head_mask(h, BLK, F32) for h in range(HL)]
    lane = lax.broadcasted_iota(jnp.int32, (BLK, 128), 1)

    def block(i, carry):
        row = pl.multiple_of(i * BLK, BLK)
        start = span_start(i)
        q = qkv_ref[pl.ds(row, BLK), :WL]
        k = qkv_ref[pl.ds(start, SPAN), WL:2 * WL]
        v = qkv_ref[pl.ds(start, SPAN), 2 * WL:]
        bias = jnp.where(segc_ref[pl.ds(row, BLK), :] == segr_ref[0:1, pl.ds(start, SPAN)], 0.0, -1e30)
        out = jnp.zeros((BLK, WL), F32)
        lse = jnp.zeros((BLK, 128), F32)
        for h in range(HL):
            s = mm(q * masks[h], k, NT) + bias
            top = jnp.max(s, axis=1, keepdims=True)
            e = jnp.exp(s - top)
            total = jnp.sum(e, axis=1, keepdims=True)
            out += mm(e.astype(BF), v) * (1.0 / total) * masks_f[h]
            lse += jnp.where(lane == h, jnp.log(total) + top, 0.0)
        o = out.astype(BF)
        o_ref[pl.ds(row, BLK), :] = o
        lse_ref[:, pl.ds(row, BLK)] = lse.T[:8, :]
        part = mm(o, wo_ref[...]).astype(BF)
        place = pl.multiple_of((i % per) * BLK, BLK)
        for j, r_ref in enumerate((r0, r1, r2, r3)):
            @pl.when((t ^ j) == i // per)
            def _():
                r_ref[pl.ds(place, BLK), :] = part
        return carry

    lax.fori_loop(0, NB, block, 0)


def full(shape):
    return pl.BlockSpec(shape, lambda *_: (0,) * len(shape))


def attn_fwd(t, pieces, w, wo, cos, sin, segc, segr):
    out_shape = (
        [jax.ShapeDtypeStruct((ROW, 3 * WL), BF), jax.ShapeDtypeStruct((ROW, WL), BF),
         jax.ShapeDtypeStruct((8, ROW), F32)]
        + [jax.ShapeDtypeStruct((PIECE, D), BF)] * TP
    )
    return pl.pallas_call(
        attn_fwd_body,
        out_shape=out_shape,
        grid_spec=pltpu.PrefetchScalarGridSpec(
            num_scalar_prefetch=1,
            grid=(1,),
            in_specs=[full((PIECE, D))] * TP + [full((D, 3 * WL)), full((WL, D)), full((ROW, 128)),
                      full((ROW, 128)), full((ROW, 1)), full((1, ROW))],
            out_specs=[full(s.shape) for s in out_shape],
        ),
        compiler_params=pltpu.CompilerParams(vmem_limit_bytes=VMEM_LIMIT),
        cost_estimate=pl.CostEstimate(flops=12 * 10**9, bytes_accessed=20 * 10**6, transcendentals=6 * 10**6),
        name="attn_fwd",
    )(t, *pieces, w, wo, cos, sin, segc, segr)


def attn_bwd_body(t_ref, g0, g1, g2, g3, wo_ref, qkv_ref, o_ref, lse_ref, cos_ref, sin_ref, segc_ref, segr_ref,
                  dp_ref, gwo_ref, do_s, dk_s, dv_s, p_s, ds_s, qm_s, dm_s):
    t = t_ref[0]
    low = lax.broadcasted_iota(jnp.int32, (BLK, 128), 1) % HEAD_DIM < HEAD_DIM // 2
    gwo = jnp.zeros((WL, D), F32)
    for j, g_ref in enumerate((g0, g1, g2, g3)):
        row = pl.multiple_of((t ^ j) * PIECE, PIECE)
        do_s[pl.ds(row, PIECE), :] = mm(g_ref[...], wo_ref[...], NT).astype(BF)
        gwo += mm(o_ref[pl.ds(row, PIECE), :], g_ref[...], TN)
    gwo_ref[...] = gwo.astype(BF)
    dk_s[...] = jnp.zeros_like(dk_s)
    dv_s[...] = jnp.zeros_like(dv_s)
    masks = [head_mask(h, BLK, BF) for h in range(HL)]
    feature = lax.broadcasted_iota(jnp.int32, (WL, BLK), 0) // HEAD_DIM

    def unrope(u, row):
        cos = cos_ref[pl.ds(row, BLK), :]
        sin = -sin_ref[pl.ds(row, BLK), :]
        return [rope_slab(u[:, s * 128:(s + 1) * 128], cos, sin, low).astype(BF) for s in range(WL // 128)]

    def block(i, carry):
        row = pl.multiple_of(i * BLK, BLK)
        start = span_start(i)
        q = qkv_ref[pl.ds(row, BLK), :WL]
        g = do_s[pl.ds(row, BLK), :]
        k = qkv_ref[pl.ds(start, SPAN), WL:2 * WL]
        v = qkv_ref[pl.ds(start, SPAN), 2 * WL:]
        bias = jnp.where(segc_ref[pl.ds(start, SPAN), :] == segr_ref[0:1, pl.ds(row, BLK)], 0.0, -1e30)
        for h in range(HL):
            qm = q * masks[h]
            gm = g * masks[h]
            cols = slice(h * BLK, (h + 1) * BLK)
            qm_s[cols, :] = qm
            dm_s[cols, :] = gm
            p = jnp.exp(mm(k, qm, NT) + bias - lse_ref[h:h + 1, pl.ds(row, BLK)])
            dp = mm(v, gm, NT)
            inner = jnp.sum(p * dp, axis=0, keepdims=True)
            p_s[:, cols] = p.astype(BF)
            ds_s[:, cols] = (p * (dp - inner)).astype(BF)
        dv_s[pl.ds(start, SPAN), :] += mm(p_s[...], dm_s[...])
        dk_s[pl.ds(start, SPAN), :] += mm(ds_s[...], qm_s[...])
        wide = mm(k, ds_s[...], TN)
        dq = jnp.zeros((WL, BLK), F32)
        for h in range(HL):
            dq += jnp.where(feature == h, wide[:, h * BLK:(h + 1) * BLK], 0.0)
        dq = (dq * (HEAD_DIM ** -0.5)).T
        for s, piece in enumerate(unrope(dq, row)):
            dp_ref[pl.ds(row, BLK), s * 128:(s + 1) * 128] = piece
        return carry

    lax.fori_loop(0, NB, block, 0)

    def finish(i, carry):
        row = pl.multiple_of(i * BLK, BLK)
        for s, piece in enumerate(unrope(dk_s[pl.ds(row, BLK), :], row)):
            dp_ref[pl.ds(row, BLK), WL + s * 128:WL + (s + 1) * 128] = piece
        dp_ref[pl.ds(row, BLK), 2 * WL:] = dv_s[pl.ds(row, BLK), :].astype(BF)
        return carry

    lax.fori_loop(0, NB, finish, 0)


def attn_bwd(t, pieces, wo, qkv, o, lse, cos, sin, segc, segr):
    out_shape = [jax.ShapeDtypeStruct((ROW, 3 * WL), BF), jax.ShapeDtypeStruct((WL, D), BF)]
    return pl.pallas_call(
        attn_bwd_body,
        out_shape=out_shape,
        grid_spec=pltpu.PrefetchScalarGridSpec(
            num_scalar_prefetch=1,
            grid=(1,),
            in_specs=[full((PIECE, D))] * TP + [full((WL, D)), full((ROW, 3 * WL)), full((ROW, WL)), full((8, ROW)),
                      full((ROW, 128)), full((ROW, 128)), full((ROW, 1)), full((1, ROW))],
            out_specs=[full(s.shape) for s in out_shape],
            scratch_shapes=[pltpu.VMEM((ROW, WL), BF), pltpu.VMEM((ROW, WL), F32), pltpu.VMEM((ROW, WL), F32),
                            pltpu.VMEM((SPAN, HL * BLK), BF), pltpu.VMEM((SPAN, HL * BLK), BF),
                            pltpu.VMEM((HL * BLK, WL), BF), pltpu.VMEM((HL * BLK, WL), BF)],
        ),
        compiler_params=pltpu.CompilerParams(vmem_limit_bytes=VMEM_LIMIT),
        cost_estimate=pl.CostEstimate(flops=20 * 10**9, bytes_accessed=20 * 10**6, transcendentals=6 * 10**6),
        name="attn_bwd",
    )(t, *pieces, wo, qkv, o, lse, cos, sin, segc, segr)


def ffn_body(ax, ay, cx, cy, w_ref, h_ref, dg_ref, dx, dy):
    i = pl.program_id(0)
    first = i < PIECE // BLK
    a = jnp.where(first, ax[...], ay[...])
    c = jnp.where(first, cx[...], cy[...])
    w_in = w_ref[:, :2 * FL]
    gate_up = mm(a, w_in)
    dh = mm(c, w_ref[:, 2 * FL:], NT)
    gate, up = gate_up[:, :FL], gate_up[:, FL:]
    sig = 1.0 / (1.0 + jnp.exp(-gate))
    act = gate * sig
    h_ref[...] = (act * up).astype(BF)
    dg_ref[:, :FL] = (dh * up * (sig * (1.0 + gate * (1.0 - sig)))).astype(BF)
    dg_ref[:, FL:] = (dh * act).astype(BF)
    da = mm(dg_ref[...], w_in, NT).astype(BF)

    @pl.when(first)
    def _():
        dx[...] = da

    @pl.when(jnp.logical_not(first))
    def _():
        dy[...] = da


def ffn(ax, ay, cx, cy, w):
    per = PIECE // BLK
    sx = pl.BlockSpec((BLK, D), lambda i: (jnp.minimum(i, per - 1), 0))
    sy = pl.BlockSpec((BLK, D), lambda i: (jnp.maximum(i - per, 0), 0))
    out_shape = [jax.ShapeDtypeStruct((2 * PIECE, FL), BF), jax.ShapeDtypeStruct((2 * PIECE, 2 * FL), BF),
                 jax.ShapeDtypeStruct((PIECE, D), BF), jax.ShapeDtypeStruct((PIECE, D), BF)]
    return pl.pallas_call(
        ffn_body,
        out_shape=out_shape,
        grid=(2 * per,),
        in_specs=[sx, sy, sx, sy, full((D, 3 * FL))],
        out_specs=[pl.BlockSpec((BLK, FL), lambda i: (i, 0)), pl.BlockSpec((BLK, 2 * FL), lambda i: (i, 0)), sx, sy],
        compiler_params=pltpu.CompilerParams(vmem_limit_bytes=VMEM_LIMIT),
        cost_estimate=pl.CostEstimate(flops=11 * 10**9, bytes_accessed=18 * 10**6, transcendentals=2 * 10**6),
        name="ffn",
    )(ax, ay, cx, cy, w)


def adam_update(weight, first_moment, second_moment, gradient, factor, use_decay, rate):
    clipped = gradient * factor
    first_new = beta_one * first_moment + (1.0 - beta_one) * clipped
    second_new = beta_two * second_moment + (1.0 - beta_two) * clipped * clipped
    first_hat = first_new / (1.0 - beta_one**STEP)
    second_hat = second_new / (1.0 - beta_two**STEP)
    direction = first_hat / (jnp.sqrt(second_hat) + adam_eps) + use_decay * weight_decay * weight
    return (clipped, weight - rate * direction, first_new, second_new)


def per_device(
    tokens, cotangent, lengths,
    qkv_master, qkv_first, qkv_second,
    out_master, out_first, out_second,
    in_master, in_first, in_second,
    down_master, down_first, down_second,
    norm_gains, gain_first, gain_second,
):
    shards = lax.axis_size("dp")
    rows = D // shards
    t = lax.axis_index("tensor").astype(jnp.int32).reshape(1)

    parts = D // WL
    out_low = out_master.astype(BF)
    out_tall = jnp.concatenate([out_low[:, j * WL:(j + 1) * WL] for j in range(parts)], axis=0)
    first = jnp.concatenate([qkv_master.reshape(rows, 3 * WL).astype(BF), out_tall], axis=1)
    second = jnp.concatenate([in_master.reshape(rows, 2 * FL).astype(BF), down_master.astype(BF)], axis=1)
    first = lax.all_gather(first, "dp", axis=0, tiled=True)
    second = lax.all_gather(second, "dp", axis=0, tiled=True)
    w_qkv = first[:, :3 * WL]
    w_out = (first[:, 3 * WL:].reshape(shards, parts, rows // parts, WL)
             .transpose(0, 2, 1, 3).reshape(WL, D))

    ends = jnp.cumsum(lengths[0])
    place_c = lax.broadcasted_iota(jnp.int32, (ROW, 1), 0)
    passed = (place_c >= ends[None, :]).astype(jnp.int32)
    segc = jnp.sum(passed, axis=1, keepdims=True)
    offset = place_c - jnp.sum(passed * lengths[0][None, :], axis=1, keepdims=True)
    place_r = lax.broadcasted_iota(jnp.int32, (1, ROW), 1)
    segr = jnp.sum((place_r >= ends[:, None]).astype(jnp.int32), axis=0, keepdims=True)
    half = HEAD_DIM // 2
    inverse = jnp.exp((jnp.arange(128) % half).astype(F32) * (-2.0 * math.log(10000.0) / HEAD_DIM))
    angles = offset.astype(F32) * inverse[None, :]
    sign = jnp.where(jnp.arange(128) % HEAD_DIM < half, -1.0, 1.0).astype(F32)
    cos, sin = jnp.cos(angles), jnp.sin(angles) * sign[None, :]

    x = tokens.astype(F32)
    a1 = gather_pieces(layer_norm(x, norm_gains[0]).astype(BF))
    cot = gather_pieces(cotangent)
    qkv, o, lse, *parts_r = attn_fwd(t, a1, w_qkv, w_out, cos, sin, segc, segr)
    middle = x + scatter_sum(*parts_r)
    a2 = gather_pieces(layer_norm(middle, norm_gains[1]).astype(BF))
    h_near, dg_near, d0, d1 = ffn(a2[0], a2[1], cot[0], cot[1], second)
    h_far, dg_far, d2, d3 = ffn(a2[2], a2[3], cot[2], cot[3], second)
    da2 = scatter_sum(d0, d1, d2, d3)

    a2_all = jnp.concatenate(a2, axis=0)
    cot_all = jnp.concatenate(cot, axis=0)
    h_all = jnp.concatenate([h_near, h_far], axis=0)
    dg_all = jnp.concatenate([dg_near, dg_far], axis=0)
    grad_down = mm(h_all, cot_all, TN).astype(BF)
    grad_in = mm(a2_all, dg_all, TN).astype(BF)
    w_down = second[:, 2 * FL:]
    outs = [mm(h[s * PIECE:(s + 1) * PIECE], w_down).astype(BF) for h in (h_near, h_far) for s in range(2)]
    layer_out = (middle + scatter_sum(*outs)).astype(BF)

    back, gain_two_grad = jax.vjp(layer_norm, middle, norm_gains[1])[1](da2)
    middle_grad = cotangent.astype(F32) + back
    g = gather_pieces(middle_grad.astype(BF))
    d_qkv, grad_out = attn_bwd(t, g, w_out, qkv, o, lse, cos, sin, segc, segr)

    a1_all = jnp.stack(a1)
    order = t[0] ^ jnp.arange(TP, dtype=jnp.int32)
    a1_row = jnp.concatenate([lax.dynamic_index_in_dim(a1_all, order[j], 0, keepdims=False) for j in range(TP)], axis=0)
    grad_qkv = mm(a1_row, d_qkv, TN).astype(BF)
    d_pieces = d_qkv.reshape(TP, PIECE, 3 * WL)
    back1 = [mm(lax.dynamic_index_in_dim(d_pieces, order[j], 0, keepdims=False), w_qkv, NT).astype(BF) for j in range(TP)]
    input_back, gain_one_grad = jax.vjp(layer_norm, x, norm_gains[0])[1](scatter_sum(*back1))
    input_grad = middle_grad + input_back

    out_tall = (grad_out.reshape(shards, rows // parts, parts, WL).transpose(0, 2, 1, 3).reshape(D, WL))
    scatter = functools.partial(lax.psum_scatter, axis_name="dp", scatter_dimension=0, tiled=True)
    red_down = scatter(grad_down).astype(F32)
    red_in = scatter(grad_in).astype(F32)
    red_first = scatter(jnp.concatenate([grad_qkv, out_tall], axis=1)).astype(F32)
    red_qkv = red_first[:, :3 * WL]
    red_out = jnp.concatenate(
        [red_first[j * (rows // parts):(j + 1) * (rows // parts), 3 * WL:] for j in range(parts)], axis=1)

    squares = (jnp.sum(red_first * red_first) + jnp.sum(red_in * red_in) + jnp.sum(red_down * red_down))
    total = jnp.stack([gain_one_grad, gain_two_grad, jnp.full((D,), squares)])
    for axis in ("tensor", "dp"):
        k = 1
        while k < lax.axis_size(axis):
            total = total + swap(total, axis, k)
            k *= 2
    gain_total = total[:2]
    grad_norm = jnp.sqrt(total[2, 0] + jnp.sum(gain_total * gain_total))
    factor = max_norm / jnp.maximum(grad_norm, max_norm)
    qkv_res = adam_update(qkv_master, qkv_first, qkv_second, red_qkv.reshape(qkv_master.shape), factor, 1.0, learn_rate)
    out_res = adam_update(out_master, out_first, out_second, red_out, factor, 1.0, learn_rate)
    in_res = adam_update(in_master, in_first, in_second, red_in.reshape(in_master.shape), factor, 1.0, learn_rate)
    down_res = adam_update(down_master, down_first, down_second, red_down, factor, 1.0, learn_rate)
    gain_res = adam_update(norm_gains, gain_first, gain_second, gain_total, factor, 0.0, gain_rate)
    return (layer_out, input_grad, *qkv_res, *out_res, *in_res, *down_res, *gain_res, grad_norm)


def solution(mesh):
    token = P(("dp", "tensor"), None)
    wide = P("dp", None, "tensor")
    tall = P(("tensor", "dp"), None)
    placed = (token, token, P("dp", None)) + (wide,) * 3 + (tall,) * 3 + (wide,) * 3 + (tall,) * 3 + (P(),) * 3
    out_specs = (token, token) + (wide,) * 4 + (tall,) * 4 + (wide,) * 4 + (tall,) * 4 + (P(),) * 5
    return jax.shard_map(per_device, mesh=mesh, in_specs=placed, out_specs=out_specs, check_vma=False)
```

time: 1110 us -> 496 us (0.45)
  waiting for transfers between devices: 510 us -> 221 us
  matrix products: 282 us -> 51.4 us
  Pallas kernels: 0 us -> 95.4 us
  blocking collectives: 76 us -> 0 us
  other arithmetic: 125 us -> 52.8 us
  local copies, waits for them, and re-layouts: 88.2 us -> 26.1 us
  starting transfers between devices: 1.2 us -> 19.6 us
    reduce_scatter x7 -> x2, waiting for transfers between devices: 295 us -> 0.02 us  [the longest x1 0.02 us: per_device(): red_in = scatter(grad_in).astype(F32)]
    dot_general x40 -> x11, matrix products: 282 us -> 51.4 us  [mm(): return lax.dot_general(a, b, dims, preferred_element_type=F32)]
    all_gather x7 -> x2, waiting for transfers between devices: 214 us -> 14.1 us  [the longest x1 14.1 us: per_device(): first = lax.all_gather(first, 'dp', axis=0, tiled=True)]
    ppermute x0 -> x29, waiting for transfers between devices: none -> 181 us  [swap(): lax.ppermute(x, axis, [(i, i ^ k) for i in range(lax.axis_size(axis))])]
    pallas_call x0 -> x4, Pallas kernels: none -> 95.4 us  [the longest x2 35 us: ffn(): pl.pallas_call(ffn_body, out_shape=out_shape, grid=(2 * per,), in_specs=[...]
    dynamic_update_slice x8 -> x0, local copies, waits for them, and re-layouts: 46.6 us -> none  [backward_row(): lax.scan(backward_block, (zeros_acc, zeros_acc), block_inputs)]
    convert_element_type x12 -> x11, other arithmetic: 54.6 us -> 12.5 us  [the longest x3 5.01 us: scatter_sum(): far = (p2.astype(F32) + swap(p3, 'tensor', 1).astype(F32)).astype(BF)]
    psum x1 -> x0, blocking collectives: 39.7 us -> none  [per_device(): lax.psum((gain_part, local_squares), ('dp', 'tensor'))]
  transfers between devices with their start and end apart: 15 -> 34, of which waited for: 13 -> 16; matrix products, arithmetic and copies ran while one was open for 32% -> 20% of each run, Pallas kernels for 0% -> 16%
where the time goes in v1:
time: 496 us; the launch traced here: 493 us
  waiting for transfers between devices  221 us (45%)
  Pallas kernels  95.4 us (19%)
  other arithmetic  52.8 us (11%)
  matrix products  51.4 us (10%)
  between operations  26.9 us (5%)
  local copies, waits for them, and re-layouts  26.1 us (5%)
  starting transfers between devices  19.6 us (4%)
    ppermute x29, waiting for transfers between devices, swap(): lax.ppermute(x, axis, [(i, i ^ k) for i in range(lax.axis_size(axis))])  181 us
    dot_general x11, matrix products, mm(): return lax.dot_general(a, b, dims, preferred_element_type=F32)  51.4 us
    pallas_call x2, Pallas kernels, ffn(): pl.pallas_call(ffn_body, out_shape=out_shape, grid=(2 * per,), in_specs=[...  35 us
    pallas_call x1, Pallas kernels, attn_bwd(): pl.pallas_call(attn_bwd_body, out_shape=out_shape, grid_spec=pltpu.Prefet...  33 us
    pallas_call x1, Pallas kernels, attn_fwd(): pl.pallas_call(attn_fwd_body, out_shape=out_shape, grid_spec=pltpu.Prefet...  27.5 us
    unnamed x6, waiting for transfers between devices  25.6 us
    ppermute x29, starting transfers between devices, swap(): lax.ppermute(x, axis, [(i, i ^ k) for i in range(lax.axis_size(axis))])  19.4 us
    all_gather x1, waiting for transfers between devices, per_device(): first = lax.all_gather(first, 'dp', axis=0, tiled=True)  14.1 us
  transfers between devices with their start and end apart: 34, of which 16 were waited for; matrix products, arithmetic and copies ran while one was open for 20% of the time, Pallas kernels for 16%

profile of v1, /device:TPU:0, one launch (start us, length us, event | category | flops | bytes accessed | tf_op | source)
XLA Modules:
  0.0 492.8 jit_solution(2581231778548924074)
XLA Ops:
  14.3 3.0 collective-permute-start.1
  17.5 23.2 %collective-permute-done.1.a2 = bf16[512,1024]{1,0:T(8,128)(2,1)} collective-permute-done((bf16[512,1024]{1,0:T(8,128)(2,1)}, bf16[512,1024]{1,0:T(8,128)(2,1)}, u32[]{:S(2)}, u32[]{:S(2)}) %collective-permute-start.1) | collective-permute-done | bytes 1048608 | tf_op jit(solution)/shard_map/ppermute | solution.py:56
  43.0 5.7 %fusion.59 = (f32[2048,128]{1,0:T(8,128)}, f32[2048,128]{1,0:T(8,128)}) fusion(f32[128]{0:T(128)S(1)} %get-tuple-element.200, f32[128]{0:T(128)S(1)} %get-tuple-element.201, f32[2048]{0:T(1024)S(1)} %subtract_convert_fusion), kind=kLoop, calls=%fused_computation.82 | loop fusion | flops 524288 | bytes 2106368 | tf_op jit(solution)/shard_map/mul | solution.py:332
  48.7 14.1 %all-gather.3.cloned.1.call-done = bf16[1024,1024]{1,0:T(8,128)(2,1)} async-done(((bf16[128,1024]{1,0:T(8,128)(2,1)}), bf16[1024,1024]{1,0:T(8,128)(2,1)}) %all-gather.3.cloned.1.call-update) | async-done | bytes 2097168 | tf_op jit(solution)/shard_map/all_gather | solution.py:315
  66.6 27.5 %attn_fwd.1 = (bf16[2048,768]{1,0:T(8,128)(2,1)}, bf16[2048,256]{1,0:T(8,128)(2,1)}, f32[8,2048]{1,0:T(8,128)}, bf16[512,1024]{1,0:T(8,128)(2,1)}, bf16[512,1024...) custom-call(s32[1]{0:T(128)} %bitcast.t_ref, bf16[512,1024]{1,0:T(8,128)(2,1)} %fusion.41.a0, ...), custom_call_target="tpu_custom_call" | custom-call | flops 12000000000 | bytes 20000000 | tf_op jit(solution)/shard_map/attn_fwd/pallas_call | solution.py:146
  94.6 2.4 collective-permute-done.4
  96.9 1.6 add_convert_fusion.4
  100.6 24.0 %collective-permute-done.5 = bf16[512,1024]{1,0:T(8,128)(2,1)S(1)} collective-permute-done((bf16[512,1024]{1,0:T(8,128)(2,1)S(1)}, bf16[512,1024]{1,0:T(8,128)(2,1)S(1)}, u32[]{:S(2)}, u32[]{:S(2)}) %collective-permute-start.5) | collective-permute-done | bytes 1048608 | tf_op jit(solution)/shard_map/ppermute | solution.py:56
  128.4 18.7 %collective-permute-done.11.cx = bf16[512,1024]{1,0:T(8,128)(2,1)S(1)} collective-permute-done((bf16[512,1024]{1,0:T(8,128)(2,1)}, bf16[512,1024]{1,0:T(8,128)(2,1)S(1)}, u32[]{:S(2)}, u32[]{:S(2)}) %collective-permute-start.11) | collective-permute-done | bytes 1048608 | tf_op jit(solution)/shard_map/ppermute | solution.py:56
  147.1 21.7 %collective-permute-done.9.ax = bf16[512,1024]{1,0:T(8,128)(2,1)S(1)} collective-permute-done((bf16[512,1024]{1,0:T(8,128)(2,1)}, bf16[512,1024]{1,0:T(8,128)(2,1)S(1)}, u32[]{:S(2)}, u32[]{:S(2)}) %collective-permute-start.9) | collective-permute-done | bytes 1048608 | tf_op jit(solution)/shard_map/ppermute | solution.py:56
  171.2 2.7 collective-permute-done.10.ay
  174.0 17.4 %ffn.3 = (bf16[1024,1024]{1,0:T(8,128)(2,1)}, bf16[1024,2048]{1,0:T(8,128)(2,1)}, bf16[512,1024]{1,0:T(8,128)(2,1)}, bf16[512,1024]{1,0:T(8,128)(2,1)}) custom-call(bf16[512,1024]{1,0:T(8,128)(2,1)} %copy-done.31, bf16[512,1024]{1,0:T(8,128)(2,1)} %collective-permute-done.10.ay, bf16[512,1024]{1,0:T(8,128)(2,1)} %copy-done.33, bf16[512,1024]{1,0:T(8,128)(2,1)} %copy-done.34, ...), custom_call_target="tpu_custom_call" | custom-call | flops 11000000512 | bytes 18000000 | tf_op jit(solution)/shard_map/ffn/pallas_call | solution.py:276
  191.3 17.6 %ffn.2 = (bf16[1024,1024]{1,0:T(8,128)(2,1)}, bf16[1024,2048]{1,0:T(8,128)(2,1)}, bf16[512,1024]{1,0:T(8,128)(2,1)}, bf16[512,1024]{1,0:T(8,128)(2,1)}) custom-call(bf16[512,1024]{1,0:T(8,128)(2,1)} %multiply_convert_fusion.ax, bf16[512,1024]{1,0:T(8,128)(2,1)} %collective-permute-done.6.ay, bf16[512,1024]{1,0:T(8,128)(2,1)} %cx.1, ...), custom_call_target="tpu_custom_call" | custom-call | flops 11000000512 | bytes 18000000 | tf_op jit(solution)/shard_map/ffn/pallas_call | solution.py:276
  209.0 9.3 %fusion.45 = bf16[1024,1024]{1,0:T(8,128)(2,1)} fusion(bf16[512,1024]{1,0:T(8,128)(2,1)} %copy-done.34, bf16[512,1024]{1,0:T(8,128)(2,1)} %copy-done.33, bf16[512,1024]{1,0:T(8,128)(2,1)} %collective-permute-done.7.cy, bf16[512,1024]{1,0:T(8,128)(2,1)} %cx.1, bf16[1024,1024]{1,0:T(8,128)(2,1)} %get-tuple-element.45, bf16[1024,1024]{1,0:T(8,128)(2,1)} %get-tuple-element.44), kind=kOutput, calls=%fused_computation.61 | convolution fusion | flops 4321181696 | bytes 10485760 | tf_op jit(solution)/shard_map/dot_general | solution.py:46
  218.9 4.3 convolution_convert_fusion.4
  223.4 12.8 %fusion.30 = bf16[1024,2048]{1,0:T(8,128)(2,1)} fusion(bf16[1024,2048]{1,0:T(8,128)(2,1)S(1)} %copy-done.38, bf16[1024,2048]{1,0:T(8,128)(2,1)S(1)} %copy-done.39, bf16[512,1024]{1,0:T(8,128)(2,1)} %collective-permute-done.10.ay, bf16[512,1024]{1,0:T(8,128)(2,1)S(1)} %copy-done.32, bf16[512,1024]{1,0:T(8,128)(2,1)} %collective-permute-done.6.ay, ...), kind=kOutput, calls=%fused_computation.31 | convolution fusion | flops 8625586176 | bytes 16777216 | tf_op jit(solution)/shard_map/dot_general | solution.py:46
  236.2 3.3 convolution_convert_fusion.6
  240.2 1.6 add_convert_fusion.1
  241.8 1.6 collective-permute-start.17
  243.5 2.9 convolution_convert_fusion.5
  246.4 1.8 add_convert_fusion.3
  248.7 2.9 convolution_convert_fusion.7
  251.6 16.3 %collective-permute-done.17 = bf16[512,1024]{1,0:T(8,128)(2,1)S(1)} collective-permute-done((bf16[512,1024]{1,0:T(8,128)(2,1)S(1)}, bf16[512,1024]{1,0:T(8,128)(2,1)S(1)}, u32[]{:S(2)}, u32[]{:S(2)}) %collective-permute-start.17) | collective-permute-done | bytes 1048608 | tf_op jit(solution)/shard_map/ppermute | solution.py:56
  267.9 2.3 multiply_reduce_fusion
  270.2 19.4 %collective-permute-done.14 = bf16[512,1024]{1,0:T(8,128)(2,1)S(1)} collective-permute-done((bf16[512,1024]{1,0:T(8,128)(2,1)S(1)}, bf16[512,1024]{1,0:T(8,128)(2,1)S(1)}, u32[]{:S(2)}, u32[]{:S(2)}) %collective-permute-start.14) | collective-permute-done | bytes 1048608 | tf_op jit(solution)/shard_map/ppermute | solution.py:56
  289.6 3.6 fusion.103
  293.3 3.3 fusion.57.g0
  298.1 23.2 %collective-permute-done.19.g2 = bf16[512,1024]{1,0:T(8,128)(2,1)} collective-permute-done((bf16[512,1024]{1,0:T(8,128)(2,1)}, bf16[512,1024]{1,0:T(8,128)(2,1)}, u32[]{:S(2)}, u32[]{:S(2)}) %collective-permute-start.19) | collective-permute-done | bytes 1048608 | tf_op jit(solution)/shard_map/ppermute | solution.py:56
  330.0 2.2 pad_maximum_fusion
  332.3 1.7 dynamic-slice_bitcast_fusion.3
  334.0 33.0 %attn_bwd.1 = (bf16[2048,768]{1,0:T(8,128)(2,1)}, bf16[256,1024]{1,0:T(8,128)(2,1)}) custom-call(s32[1]{0:T(128)} %bitcast.t_ref, bf16[512,1024]{1,0:T(8,128)(2,1)} %fusion.57.g0, bf16[512,1024]{1,0:T(8,128)(2,1)} %collective-permute-done.18.g1, bf16[512,1024]{1,0:T(8,128)(2,1)} %collective-permute-done.19.g2, bf16[512,1024]{1,0:T(8,128)(2,1)} %collective-permute-done.20.g3, ...), custom_call_target="tpu_custom_call" | custom-call | flops 20000000000 | bytes 20000000 | tf_op jit(solution)/shard_map/attn_bwd/pallas_call | solution.py:226
  369.6 6.4 %fusion.50 = bf16[1024,768]{0,1:T(8,128)(2,1)S(1)} fusion(bf16[2048,768]{1,0:T(8,128)(2,1)} %get-tuple-element.53, bf16[512,1024]{1,0:T(8,128)(2,1)} %get-tuple-element.178, bf16[512,1024]{1,0:T(8,128)(2,1)} %get-tuple-element.179, bf16[512,1024]{1,0:T(8,128)(2,1)} %get-tuple-element.180, bf16[512,1024]{1,0:T(8,128)(2,1)S(1)} %get-tuple-element.177), kind=kOutput, calls=%fused_computation.62 | convolution fusion | flops 3238789120 | bytes 8912896 | tf_op jit(solution)/shard_map/dot_general | solution.py:46
  376.2 2.8 copy.109
  380.6 2.3 convolution_convert_fusion
  383.5 2.0 convolution_convert_fusion.2
  385.8 2.0 add_convert_fusion
  389.2 1.7 fusion.75
  390.9 22.7 %collective-permute-done.23 = bf16[512,1024]{1,0:T(8,128)(2,1)} collective-permute-done((bf16[512,1024]{1,0:T(8,128)(2,1)}, bf16[512,1024]{1,0:T(8,128)(2,1)}, u32[]{:S(2)}, u32[]{:S(2)}) %collective-permute-start.23) | collective-permute-done | bytes 1048608 | tf_op jit(solution)/shard_map/ppermute | solution.py:56
  413.5 3.1 fusion.44
  419.1 1.9 fusion.58
  421.0 25.5 %reduce-scatter.10.cloned.1.call-done = bf16[128,1024]{1,0:T(8,128)(2,1)} async-done(((bf16[1024,1024]{1,0:T(8,128)(2,1)}), bf16[128,1024]{1,0:T(8,128)(2,1)}) %reduce-scatter.10.cloned.1.call-update) | async-done | bytes 262160
  453.2 2.3 collective-permute-done.25
  456.3 3.0 collective-permute-done.26
  460.2 4.1 add_add_fusion.2
  464.3 1.8 collective-permute-start.28
  473.6 1.6 multiply_subtract_fusion.4
  475.2 2.4 multiply_subtract_fusion.2
  477.8 4.8 multiply_subtract_fusion
  (203 shorter events, 50.4 us)
Async XLA Ops:
  7.2 55.5 %all-gather.3.cloned.1.call-start = ((), (), s32[]{:S(2)}) async-start(), calls=%async_computation.3 | async-start | bytes 2359296 | tf_op jit(solution)/shard_map/all_gather | solution.py:315
  10.4 163.6 %all-gather.5.cloned.1.call-start = ((), (), s32[]{:S(2)}) async-start(), calls=%async_computation.4 | async-start | bytes 7077888 | tf_op jit(solution)/shard_map/all_gather | solution.py:316
  12.0 5.3 %copy-start.30 = (s32[1,16]{1,0:T(1,128)S(1)}, s32[1,16]{1,0:T(1,128)}, u32[]{:S(2)}) copy-start(s32[1,16]{1,0:T(1,128)} %param.20) | copy-start | bytes 196
  12.0 377.2 %reduce-scatter.8.cloned.1.call-start = ((), (), s32[]{:S(2)}) async-start(), calls=%async_computation.6 | async-start | bytes 2359296 | tf_op jit(solution)/shard_map/reduce_scatter | solution.py:370
  14.3 26.4 %collective-permute-start.1 = (bf16[512,1024]{1,0:T(8,128)(2,1)}, bf16[512,1024]{1,0:T(8,128)(2,1)}, u32[]{:S(2)}, u32[]{:S(2)}) collective-permute-start(bf16[512,1024]{1,0:T(8,128)(2,1)} %fusion.41.a0), channel_id=1, source_target_pairs={{0,2},{1,3},{2,0},{3,1},{4,6},{5,7},{6,4},{7,5},{8,10},{9,11},{10,... | collective-permute-start | bytes 3145736 | tf_op jit(solution)/shard_map/ppermute | solution.py:56
  17.3 49.3 %collective-permute-start = (bf16[512,1024]{1,0:T(8,128)(2,1)}, bf16[512,1024]{1,0:T(8,128)(2,1)}, u32[]{:S(2)}, u32[]{:S(2)}) collective-permute-start(bf16[512,1024]{1,0:T(8,128)(2,1)} %fusion.41.a0), channel_id=1, source_target_pairs={{0,1},{1,0},{2,3},{3,2},{4,5},{5,4},{6,7},{7,6},{8,9},{9,8},{10,11... | collective-permute-start | bytes 3145736 | tf_op jit(solution)/shard_map/ppermute | solution.py:56
  40.8 25.8 %collective-permute-start.2 = (bf16[512,1024]{1,0:T(8,128)(2,1)}, bf16[512,1024]{1,0:T(8,128)(2,1)}, u32[]{:S(2)}, u32[]{:S(2)}) collective-permute-start(bf16[512,1024]{1,0:T(8,128)(2,1)} %collective-permute-done.1.a2), channel_id=1, source_target_pairs={{0,1},{1,0},{2,3},{3,2},{4,5},{5,4},{6,7},{7,6},{8,9},{9,8},{10,11... | collective-permute-start | bytes 3145736 | tf_op jit(solution)/shard_map/ppermute | solution.py:56
  94.0 30.6 %copy-start.19 = (bf16[512,1024]{1,0:T(8,128)(2,1)S(1)}, bf16[512,1024]{1,0:T(8,128)(2,1)}, u32[]{:S(2)}) copy-start(bf16[512,1024]{1,0:T(8,128)(2,1)} %get-tuple-element.40) | copy-start | bytes 3145732
  94.0 2.9 collective-permute-start.4
  94.1 6.6 %collective-permute-start.3 = (bf16[512,1024]{1,0:T(8,128)(2,1)}, bf16[512,1024]{1,0:T(8,128)(2,1)S(1)}, u32[]{:S(2)}, u32[]{:S(2)}) collective-permute-start(bf16[512,1024]{1,0:T(8,128)(2,1)} %get-tuple-element.41), channel_id=1, source_target_pairs={{0,1},{1,0},{2,3},{3,2},{4,5},{5,4},{6,7},{7,6},{8,9},{9,8},{10,11... | collective-permute-start | bytes 3145736 | tf_op jit(solution)/shard_map/ppermute | solution.py:56
  98.5 26.1 %collective-permute-start.5 = (bf16[512,1024]{1,0:T(8,128)(2,1)S(1)}, bf16[512,1024]{1,0:T(8,128)(2,1)S(1)}, u32[]{:S(2)}, u32[]{:S(2)}) collective-permute-start(bf16[512,1024]{1,0:T(8,128)(2,1)S(1)} %add_convert_fusion.4), channel_id=1, source_target_pairs={{0,2},{1,3},{2,0},{3,1},{4,6},{5,7},{6,4},{7,5},{8,10},{9,11},{10,... | collective-permute-start | bytes 3145736 | tf_op jit(solution)/shard_map/ppermute | solution.py:56
  100.1 47.0 %collective-permute-start.11 = (bf16[512,1024]{1,0:T(8,128)(2,1)}, bf16[512,1024]{1,0:T(8,128)(2,1)S(1)}, u32[]{:S(2)}, u32[]{:S(2)}) collective-permute-start(bf16[512,1024]{1,0:T(8,128)(2,1)} %cx.1), channel_id=1, source_target_pairs={{0,2},{1,3},{2,0},{3,1},{4,6},{5,7},{6,4},{7,5},{8,10},{9,11},{10,... | collective-permute-start | bytes 3145736 | tf_op jit(solution)/shard_map/ppermute | solution.py:56
  126.9 41.8 %collective-permute-start.9 = (bf16[512,1024]{1,0:T(8,128)(2,1)}, bf16[512,1024]{1,0:T(8,128)(2,1)S(1)}, u32[]{:S(2)}, u32[]{:S(2)}) collective-permute-start(bf16[512,1024]{1,0:T(8,128)(2,1)} %multiply_convert_fusion.ax), channel_id=1, source_target_pairs={{0,2},{1,3},{2,0},{3,1},{4,6},{5,7},{6,4},{7,5},{8,10},{9,11},{10,... | collective-permute-start | bytes 3145736 | tf_op jit(solution)/shard_map/ppermute | solution.py:56
  147.1 22.6 %copy-start.33 = (bf16[512,1024]{1,0:T(8,128)(2,1)}, bf16[512,1024]{1,0:T(8,128)(2,1)S(1)}, u32[]{:S(2)}) copy-start(bf16[512,1024]{1,0:T(8,128)(2,1)S(1)} %collective-permute-done.11.cx) | copy-start | bytes 3145732
  147.1 23.2 %collective-permute-start.12 = (bf16[512,1024]{1,0:T(8,128)(2,1)S(1)}, bf16[512,1024]{1,0:T(8,128)(2,1)S(1)}, u32[]{:S(2)}, u32[]{:S(2)}) collective-permute-start(bf16[512,1024]{1,0:T(8,128)(2,1)S(1)} %collective-permute-done.11.cx), channel_id=1, source_target_pairs={{0,1},{1,0},{2,3},{3,2},{4,5},{5,4},{6,7},{7,6},{8,9},{9,8},{10,11... | collective-permute-start | bytes 3145736 | tf_op jit(solution)/shard_map/ppermute | solution.py:56
  169.7 4.2 collective-permute-start.10
  169.7 21.6 %collective-permute-start.7 = (bf16[512,1024]{1,0:T(8,128)(2,1)}, bf16[512,1024]{1,0:T(8,128)(2,1)}, u32[]{:S(2)}, u32[]{:S(2)}) collective-permute-start(bf16[512,1024]{1,0:T(8,128)(2,1)} %cx.1), channel_id=1, source_target_pairs={{0,1},{1,0},{2,3},{3,2},{4,5},{5,4},{6,7},{7,6},{8,9},{9,8},{10,11... | collective-permute-start | bytes 3145736 | tf_op jit(solution)/shard_map/ppermute | solution.py:56
  170.2 21.1 %collective-permute-start.6 = (bf16[512,1024]{1,0:T(8,128)(2,1)}, bf16[512,1024]{1,0:T(8,128)(2,1)}, u32[]{:S(2)}, u32[]{:S(2)}) collective-permute-start(bf16[512,1024]{1,0:T(8,128)(2,1)} %multiply_convert_fusion.ax), channel_id=1, source_target_pairs={{0,1},{1,0},{2,3},{3,2},{4,5},{5,4},{6,7},{7,6},{8,9},{9,8},{10,11... | collective-permute-start | bytes 3145736 | tf_op jit(solution)/shard_map/ppermute | solution.py:56
  218.3 200.8 %reduce-scatter.6.cloned.1.call-start = ((), (), s32[]{:S(2)}) async-start(), calls=%async_computation.5 | async-start | bytes 4718592 | tf_op jit(solution)/shard_map/reduce_scatter | solution.py:371
  218.3 21.9 %collective-permute-start.16 = (bf16[512,1024]{1,0:T(8,128)(2,1)}, bf16[512,1024]{1,0:T(8,128)(2,1)}, u32[]{:S(2)}, u32[]{:S(2)}) collective-permute-start(bf16[512,1024]{1,0:T(8,128)(2,1)} %get-tuple-element.49), channel_id=1, source_target_pairs={{0,1},{1,0},{2,3},{3,2},{4,5},{5,4},{6,7},{7,6},{8,9},{9,8},{10,11... | collective-permute-start | bytes 3145736 | tf_op jit(solution)/shard_map/ppermute | solution.py:56
  218.5 33.1 %collective-permute-start.15 = (bf16[512,1024]{1,0:T(8,128)(2,1)}, bf16[512,1024]{1,0:T(8,128)(2,1)}, u32[]{:S(2)}, u32[]{:S(2)}) collective-permute-start(bf16[512,1024]{1,0:T(8,128)(2,1)} %get-tuple-element.47), channel_id=1, source_target_pairs={{0,1},{1,0},{2,3},{3,2},{4,5},{5,4},{6,7},{7,6},{8,9},{9,8},{10,11... | collective-permute-start | bytes 3145736 | tf_op jit(solution)/shard_map/ppermute | solution.py:56
  223.3 23.1 %collective-permute-start.13 = (bf16[512,1024]{1,0:T(8,128)(2,1)}, bf16[512,1024]{1,0:T(8,128)(2,1)}, u32[]{:S(2)}, u32[]{:S(2)}) collective-permute-start(bf16[512,1024]{1,0:T(8,128)(2,1)} %convolution_convert_fusion.4), channel_id=1, source_target_pairs={{0,1},{1,0},{2,3},{3,2},{4,5},{5,4},{6,7},{7,6},{8,9},{9,8},{10,11... | collective-permute-start | bytes 3145736 | tf_op jit(solution)/shard_map/ppermute | solution.py:56
  236.2 210.3 %reduce-scatter.10.cloned.1.call-start = ((), (), s32[]{:S(2)}) async-start(), calls=%async_computation.7 | async-start | bytes 2359296
  239.6 30.6 %collective-permute-start.8 = (bf16[512,1024]{1,0:T(8,128)(2,1)S(1)}, bf16[512,1024]{1,0:T(8,128)(2,1)S(1)}, u32[]{:S(2)}, u32[]{:S(2)}) collective-permute-start(bf16[512,1024]{1,0:T(8,128)(2,1)S(1)} %convolution_convert_fusion.6), channel_id=1, source_target_pairs={{0,1},{1,0},{2,3},{3,2},{4,5},{5,4},{6,7},{7,6},{8,9},{9,8},{10,11... | collective-permute-start | bytes 3145736 | tf_op jit(solution)/shard_map/ppermute | solution.py:56
  241.8 26.1 %collective-permute-start.17 = (bf16[512,1024]{1,0:T(8,128)(2,1)S(1)}, bf16[512,1024]{1,0:T(8,128)(2,1)S(1)}, u32[]{:S(2)}, u32[]{:S(2)}) collective-permute-start(bf16[512,1024]{1,0:T(8,128)(2,1)S(1)} %add_convert_fusion.1), channel_id=1, source_target_pairs={{0,2},{1,3},{2,0},{3,1},{4,6},{5,7},{6,4},{7,5},{8,10},{9,11},{10,... | collective-permute-start | bytes 3145736 | tf_op jit(solution)/shard_map/ppermute | solution.py:56
  248.1 19.8 %copy-start.7 = (bf16[512,1024]{1,0:T(8,128)(2,1)S(1)}, bf16[512,1024]{1,0:T(8,128)(2,1)}, u32[]{:S(2)}) copy-start(bf16[512,1024]{1,0:T(8,128)(2,1)} %get-tuple-element.46) | copy-start | bytes 3145732
  248.1 41.5 %collective-permute-start.14 = (bf16[512,1024]{1,0:T(8,128)(2,1)S(1)}, bf16[512,1024]{1,0:T(8,128)(2,1)S(1)}, u32[]{:S(2)}, u32[]{:S(2)}) collective-permute-start(bf16[512,1024]{1,0:T(8,128)(2,1)S(1)} %add_convert_fusion.3), channel_id=1, source_target_pairs={{0,2},{1,3},{2,0},{3,1},{4,6},{5,7},{6,4},{7,5},{8,10},{9,11},{10,... | collective-permute-start | bytes 3145736 | tf_op jit(solution)/shard_map/ppermute | solution.py:56
  296.6 24.7 %collective-permute-start.19 = (bf16[512,1024]{1,0:T(8,128)(2,1)}, bf16[512,1024]{1,0:T(8,128)(2,1)}, u32[]{:S(2)}, u32[]{:S(2)}) collective-permute-start(bf16[512,1024]{1,0:T(8,128)(2,1)} %fusion.57.g0), channel_id=1, source_target_pairs={{0,2},{1,3},{2,0},{3,1},{4,6},{5,7},{6,4},{7,5},{8,10},{9,11},{10,... | collective-permute-start | bytes 3145736 | tf_op jit(solution)/shard_map/ppermute | solution.py:56
  298.1 35.9 %collective-permute-start.18 = (bf16[512,1024]{1,0:T(8,128)(2,1)}, bf16[512,1024]{1,0:T(8,128)(2,1)}, u32[]{:S(2)}, u32[]{:S(2)}) collective-permute-start(bf16[512,1024]{1,0:T(8,128)(2,1)} %fusion.57.g0), channel_id=1, source_target_pairs={{0,1},{1,0},{2,3},{3,2},{4,5},{5,4},{6,7},{7,6},{8,9},{9,8},{10,11... | collective-permute-start | bytes 3145736 | tf_op jit(solution)/shard_map/ppermute | solution.py:56
  321.3 12.7 %collective-permute-start.20 = (bf16[512,1024]{1,0:T(8,128)(2,1)}, bf16[512,1024]{1,0:T(8,128)(2,1)}, u32[]{:S(2)}, u32[]{:S(2)}) collective-permute-start(bf16[512,1024]{1,0:T(8,128)(2,1)} %collective-permute-done.19.g2), channel_id=1, source_target_pairs={{0,1},{1,0},{2,3},{3,2},{4,5},{5,4},{6,7},{7,6},{8,9},{9,8},{10,11... | collective-permute-start | bytes 3145736 | tf_op jit(solution)/shard_map/ppermute | solution.py:56
  369.6 6.4 %copy-start.13 = (bf16[1024,256]{0,1:T(8,128)(2,1)S(1)}, bf16[1024,256]{0,1:T(8,128)(2,1)}, u32[]{:S(2)}) copy-start(bf16[1024,256]{0,1:T(8,128)(2,1)} %copy.100) | copy-start | bytes 1572868
  382.9 2.9 collective-permute-start.22
  385.5 5.4 %collective-permute-start.21 = (bf16[512,1024]{1,0:T(8,128)(2,1)}, bf16[512,1024]{1,0:T(8,128)(2,1)}, u32[]{:S(2)}, u32[]{:S(2)}) collective-permute-start(bf16[512,1024]{1,0:T(8,128)(2,1)} %convolution_convert_fusion.2), channel_id=1, source_target_pairs={{0,1},{1,0},{2,3},{3,2},{4,5},{5,4},{6,7},{7,6},{8,9},{9,8},{10,11... | collective-permute-start | bytes 3145736 | tf_op jit(solution)/shard_map/ppermute | solution.py:56
  387.8 25.8 %collective-permute-start.23 = (bf16[512,1024]{1,0:T(8,128)(2,1)}, bf16[512,1024]{1,0:T(8,128)(2,1)}, u32[]{:S(2)}, u32[]{:S(2)}) collective-permute-start(bf16[512,1024]{1,0:T(8,128)(2,1)} %add_convert_fusion), channel_id=1, source_target_pairs={{0,2},{1,3},{2,0},{3,1},{4,6},{5,7},{6,4},{7,5},{8,10},{9,11},{10,... | collective-permute-start | bytes 3145736 | tf_op jit(solution)/shard_map/ppermute | solution.py:56
  418.0 42.1 %copy-start.2 = (f32[512,1024]{1,0:T(8,128)S(1)}, f32[512,1024]{1,0:T(8,128)}, u32[]{:S(2)}) copy-start(f32[512,1024]{1,0:T(8,128)} %copy-done.1) | copy-start | bytes 6291460
  450.5 1.2 collective-permute-start.24
  451.8 3.7 collective-permute-start.25
  455.6 3.7 collective-permute-start.26
  459.3 5.0 %collective-permute-start.27 = (f32[3,1024]{1,0:T(4,128)S(1)}, f32[3,1024]{1,0:T(4,128)S(1)}, u32[]{:S(2)}, u32[]{:S(2)}) collective-permute-start(f32[3,1024]{1,0:T(4,128)S(1)} %add.239), channel_id=1, source_target_pairs={{0,8},{4,12},{8,0},{12,4},{16,24},{20,28},{24,16},{28,20},{1,9},{5... | collective-permute-start | bytes 36872 | tf_op jit(solution)/shard_map/ppermute | solution.py:56
  464.3 8.2 %copy-start.12 = (bf16[128,2048]{1,0:T(8,128)(2,1)S(1)}, bf16[128,2048]{1,0:T(8,128)(2,1)}, u32[]{:S(2)}) copy-start(bf16[128,2048]{1,0:T(8,128)(2,1)} %reduce-scatter.6.cloned.1.call-done) | copy-start | bytes 1572868
  464.3 4.7 collective-permute-start.28
  472.6 5.0 %copy-start.5 = (f32[128,2,1024]{2,1,0:T(2,128)S(1)}, f32[128,2,1024]{2,1,0:T(2,128)}, u32[]{:S(2)}) copy-start(f32[128,2,1024]{2,1,0:T(2,128)} %param.27) | copy-start | bytes 3145732
  473.5 9.0 %copy-start.6 = (f32[128,2,1024]{2,1,0:T(2,128)}, f32[128,2,1024]{2,1,0:T(2,128)S(1)}, u32[]{:S(2)}) copy-start(f32[128,2,1024]{2,1,0:T(2,128)S(1)} %mul.449) | copy-start | bytes 3145732
  477.7 4.9 copy-start.22
  477.7 5.7 %copy-start.9 = (f32[128,1024]{1,0:T(8,128)S(1)}, f32[128,1024]{1,0:T(8,128)}, u32[]{:S(2)}) copy-start(f32[128,1024]{1,0:T(8,128)} %param.30) | copy-start | bytes 1572868
  477.8 5.7 %copy-start.18 = (bf16[128,1024]{1,0:T(8,128)(2,1)S(1)}, bf16[128,1024]{1,0:T(8,128)(2,1)}, u32[]{:S(2)}) copy-start(bf16[128,1024]{1,0:T(8,128)(2,1)} %reduce-scatter.8.cloned.1.call-done) | copy-start | bytes 786436
  477.8 5.7 %copy-start.20 = (f32[128,1024]{1,0:T(8,128)S(1)}, f32[128,1024]{1,0:T(8,128)}, u32[]{:S(2)}) copy-start(f32[128,1024]{1,0:T(8,128)} %param.31) | copy-start | bytes 1572868
  477.8 5.7 %copy-start.21 = (f32[128,1024]{1,0:T(8,128)S(1)}, f32[128,1024]{1,0:T(8,128)}, u32[]{:S(2)}) copy-start(f32[128,1024]{1,0:T(8,128)} %param.32) | copy-start | bytes 1572868
  (26 other events, 89.6 us)
Sparse Core Ops, SparseCore 0:
  10.7 51.9 all-gather.2
  64.9 97.5 all-gather.4
  218.4 66.2 reduce-scatter.7
  288.2 86.8 reduce-scatter.5
  379.1 67.3 reduce-scatter.9
